TPU v7x, 128 devices: a whole 4x4x4 slice. The times are simulated.
128 devices in a mesh: row: 16 (over x, y_lo, core), col: 8 (over y_hi, z).
Axes of the slice: x: 4, y: 4 (y_hi: 2, y_lo: 2; y = y_hi * 2 + y_lo), z: 4, core: 2. Of those that a mesh axis runs over, the one named last changes fastest.
Arguments:
- coarse_feats: bfloat16 [64, 1024], P(None, ('row', 'col')), may hold values from -6 to 6
- fine_feats: bfloat16 [64, 1024], P(None, ('row', 'col')), may hold values from -6 to 6
- pair_prior: bfloat16 [64, 1024, 1024], P(None, 'row', 'col'), may hold values from -6 to 6
- zoom_start: int32 [2], replicated, may hold values from 0 to 512, as said below
- coarse_weights: bfloat16 [2, 3, 64, 192], replicated, may hold values from -0.25 to 0.25
- coarse_bias: float32 [2, 64], replicated, may hold values from -2.5 to 2.5
- refine_first: bfloat16 [3, 64, 384], replicated, may hold values from -0.1875 to 0.1875
- refine_second: bfloat16 [3, 64, 192], replicated, may hold values from -0.25 to 0.25
- refine_bias: float32 [2, 64], replicated, may hold values from -2.5 to 2.5
Outputs:
- coarse_map: bfloat16 [64, 1024, 1024], P(None, 'row', 'col')
- refined: bfloat16 [64, 1024, 1024], P(None, 'row', 'col')
Inputs may be any that keep to these rules, and one draw needn't show every extreme that they name: `zoom_start`: the two entries are 0 and 512 in either order.
All inputs are finite; a program needn't handle non-finite values.
Results may differ from a plain program's by a relative error of at most 0.0059.
Values may be sent and summed in bfloat16 or wider, within the bound.
A program may use at most 64 MiB of HBM per device.

v0:
```python
import jax
import jax.numpy as jnp
from jax import lax
from jax.sharding import PartitionSpec as P

margin_bins = 24


def with_halo(block, sides, width):
    for axis, dim in sides:
        count = lax.axis_size(axis)
        forward = [(i, i + 1) for i in range(count - 1)]
        backward = [(target, source) for source, target in forward]
        low = lax.ppermute(
            lax.slice_in_dim(block, block.shape[dim] - width, None, axis=dim), axis, forward
        )
        high = lax.ppermute(lax.slice_in_dim(block, 0, width, axis=dim), axis, backward)
        block = jnp.concatenate([low, block, high], axis=dim)
    return block


def conv_valid(padded, weights, spacing, out_rows, out_cols):
    inputs = padded.shape[0]
    outputs = weights.shape[1]
    summed = jnp.zeros((outputs, out_rows * out_cols), jnp.float32)
    for tap_row in range(3):
        strip = padded[:, tap_row * spacing : tap_row * spacing + out_rows, :]
        slices = [
            strip[:, :, tap_col * spacing : tap_col * spacing + out_cols] for tap_col in range(3)
        ]
        if 3 * inputs <= 256:
            stacked = jnp.concatenate(slices, axis=0).reshape(3 * inputs, out_rows * out_cols)
            summed = summed + jnp.dot(weights[tap_row], stacked, preferred_element_type=jnp.float32)
        else:
            for tap_col in range(3):
                kernel = weights[tap_row][:, tap_col * inputs : (tap_col + 1) * inputs]
                summed = summed + jnp.dot(
                    kernel,
                    slices[tap_col].reshape(inputs, out_rows * out_cols),
                    preferred_element_type=jnp.float32,
                )
    return summed.reshape(outputs, out_rows, out_cols)


def conv_layer(padded, weights, biases, spacing, out_rows, out_cols):
    result = conv_valid(padded, weights, spacing, out_rows, out_cols)
    return jnp.maximum(result + biases[:, None, None], 0.0)


def pair_sum(padded_feats, row_first, col_first, row_extent, col_extent):
    row_part = lax.dynamic_slice_in_dim(
        padded_feats, row_first + margin_bins, row_extent, 1
    ).astype(jnp.float32)
    col_part = lax.dynamic_slice_in_dim(
        padded_feats, col_first + margin_bins, col_extent, 1
    ).astype(jnp.float32)
    return row_part[:, :, None] + col_part[:, None, :]


def inside_grid(row_first, col_first, row_extent, col_extent, bins_side):
    row_ids = row_first + jnp.arange(row_extent, dtype=jnp.int32)
    col_ids = col_first + jnp.arange(col_extent, dtype=jnp.int32)
    row_inside = (row_ids >= 0) & (row_ids < bins_side)
    col_inside = (col_ids >= 0) & (col_ids < bins_side)
    return (row_inside[:, None] & col_inside[None, :])[None]


def direct_move(source, axis_dim, extent, position, offset, sender):
    length = source.shape[axis_dim]
    layout = source.shape[:axis_dim] + (2, length // 2) + source.shape[axis_dim + 1 :]
    halves = jnp.moveaxis(source.reshape(layout), axis_dim, 0)
    targets = jnp.arange(extent, dtype=jnp.int32)
    owners = offset + targets // 2
    chosen = jnp.take(halves, targets % 2, axis=0)
    keeping = (owners == position).reshape((extent,) + (1,) * source.ndim)
    outgoing = jnp.where(keeping, chosen, jnp.zeros_like(chosen))
    incoming = sender(outgoing)
    return lax.dynamic_index_in_dim(incoming, offset + position // 2, 0, keepdims=False)


def per_device(
    coarse_feats,
    fine_feats,
    pair_prior,
    zoom_start,
    coarse_weights,
    coarse_bias,
    refine_first,
    refine_second,
    refine_bias,
):
    channels, tile_rows, tile_cols = pair_prior.shape
    row_count = lax.axis_size("row")
    col_count = lax.axis_size("col")
    bins_side = tile_rows * row_count
    row_place = lax.axis_index("row")
    col_place = lax.axis_index("col")
    row_start = row_place * tile_rows
    col_start = col_place * tile_cols
    coarse_all, fine_all = (
        lax.all_gather(coarse_feats, ("row", "col"), axis=1, tiled=True),
        lax.all_gather(fine_feats, ("row", "col"), axis=1, tiled=True),
    )
    coarse_padded = jnp.pad(coarse_all, ((0, 0), (margin_bins, margin_bins)))
    fine_padded = jnp.pad(fine_all, ((0, 0), (margin_bins, margin_bins)))
    pair_map = (
        pair_sum(coarse_padded, row_start, col_start, tile_rows, tile_cols)
        + pair_prior.astype(jnp.float32)
    ).astype(jnp.bfloat16)
    padded = with_halo(pair_map, (("row", 1), ("col", 2)), 2)
    hidden_coarse = conv_layer(
        padded, coarse_weights[0], coarse_bias[0], 2, tile_rows, tile_cols
    ).astype(jnp.bfloat16)
    padded = with_halo(hidden_coarse, (("row", 1), ("col", 2)), 4)
    coarse_map = conv_layer(
        padded, coarse_weights[1], coarse_bias[1], 4, tile_rows, tile_cols
    ).astype(jnp.bfloat16)
    zoom_bin = zoom_start[0]
    col_offset = zoom_bin // tile_cols
    row_offset = zoom_bin // tile_rows
    narrowed = direct_move(
        coarse_map,
        2,
        col_count,
        col_place,
        col_offset,
        lambda outgoing: lax.all_to_all(outgoing, "col", split_axis=0, concat_axis=0, tiled=True),
    )
    window = direct_move(
        narrowed,
        1,
        row_count,
        row_place,
        row_offset,
        lambda outgoing: lax.all_to_all(outgoing, "row", split_axis=0, concat_axis=0, tiled=True),
    )
    upsampled = jnp.broadcast_to(
        window[:, :, None, :, None], (channels, tile_rows // 2, 2, tile_cols // 2, 2)
    ).reshape(channels, tile_rows, tile_cols)
    window_padded = with_halo(upsampled, (("row", 1), ("col", 2)), 8)
    inside = inside_grid(row_start - 8, col_start - 8, tile_rows + 16, tile_cols + 16, bins_side)
    fine_pair = jnp.where(
        inside,
        pair_sum(fine_padded, row_start - 8, col_start - 8, tile_rows + 16, tile_cols + 16),
        0.0,
    ).astype(jnp.bfloat16)
    joined = jnp.concatenate([window_padded, fine_pair], axis=0)
    hidden_refine = conv_layer(
        joined, refine_first, refine_bias[0], 8, tile_rows, tile_cols
    ).astype(jnp.bfloat16)
    padded = with_halo(hidden_refine, (("row", 1), ("col", 2)), 16)
    refined = conv_layer(padded, refine_second, refine_bias[1], 16, tile_rows, tile_cols).astype(
        jnp.bfloat16
    )
    return (coarse_map, refined)


def solution(mesh):
    return jax.shard_map(
        per_device,
        mesh=mesh,
        in_specs=(
            P(None, ("row", "col")),
            P(None, ("row", "col")),
            P(None, "row", "col"),
            P(),
            P(),
            P(),
            P(),
            P(),
            P(),
        ),
        out_specs=(P(None, "row", "col"), P(None, "row", "col")),
        check_vma=False,
    )
```

profile of v0, /device:TPU:1, one launch (start us, length us, event | category | flops | bytes accessed | tf_op | source)
XLA Modules:
  0.0 1004.3 jit_solution(12770333739575595750)
XLA Ops:
  0.6 305.8 %all_gather.6 = bf16[64,1024]{0,1:T(8,128)(2,1)S(1)} all-gather(bf16[64,8]{0,1:T(8,128)(2,1)} %param.9), channel_id=1, replica_groups=mesh['row'=16,'col'=8] {'row','col'}, dimensions={1}, use_global_device_ids=true | all-gather | bytes 132096 | tf_op jit(solution)/shard_map/all_gather | solution.py:101
  308.9 17.2 %collective-permute-start.1 = (bf16[64,2,128]{2,0,1:T(8,128)(2,1)S(1)}, bf16[64,2,128]{2,0,1:T(8,128)(2,1)S(1)}, u32[]{:S(2)}, u32[]{:S(2)}) collective-permute-start(bf16[64,2,128]{2,0,1:T(8,128)(2,1)S(1)} %get-tuple-element.68), channel_id=1, source_target_pairs={{8,0},{16,8},{24,16},{32,24},{40,32},{48,40},{56,48},{64,56},{72,6... | collective-permute-start | bytes 98312 | tf_op jit(solution)/shard_map/ppermute | solution.py:17
  344.5 8.5 fusion.37
  355.6 3.2 collective-permute-start.5
  358.9 3.9 collective-permute-start.4
  382.5 9.4 fusion.31
  394.2 4.4 reshape.256
  401.3 4.6 gather_fusion
  405.9 7.9 select_select_fusion.1
  413.8 10.5 %reshape.289 = bf16[8,2,131072]{2,1,0:T(2,128)(2,1)} reshape(bf16[8,64,64,64]{3,2,1,0:T(8,128)(2,1)} %select_select_fusion.1) | data formatting | bytes 8388608
  424.2 6.4 all-to-all-start
  430.8 49.3 %all-to-all-done = bf16[8,2,131072]{2,1,0:T(2,128)(2,1)} async-done(((bf16[8,2,131072]{2,1,0:T(2,128)(2,1)}), bf16[8,2,131072]{2,1,0:T(2,128)(2,1)}, u32[]{:S(2)}, u32[]{:S(2)}) %all-to-all-start) | async-done | bytes 4194336 | tf_op jit(solution)/shard_map/all_to_all | solution.py:127
  480.1 10.3 %reshape.290 = bf16[8,64,64,64]{3,2,1,0:T(8,128)(2,1)} reshape(bf16[8,2,131072]{2,1,0:T(2,128)(2,1)} %all-to-all-done) | data formatting | bytes 8388608
  491.7 4.7 gather_fusion.1
  496.3 7.9 select_select_fusion
  504.2 14.0 %reshape.291 = bf16[16,2,65536]{2,1,0:T(2,128)(2,1)} reshape(bf16[16,64,32,64]{3,2,1,0:T(8,128)(2,1)} %select_select_fusion) | data formatting | bytes 8388608
  518.2 4.9 all-to-all-start.1
  523.1 342.9 %all_gather.7 = bf16[64,1024]{0,1:T(8,128)(2,1)S(1)} all-gather(bf16[64,8]{0,1:T(8,128)(2,1)S(1)} %copy-done.11), channel_id=1, replica_groups=mesh['row'=16,'col'=8] {'row','col'}, dimensions={1}, use_global_device_ids=true | all-gather | bytes 132096 | tf_op jit(solution)/shard_map/all_gather | solution.py:102
  868.6 13.6 %reshape.292 = bf16[16,64,32,64]{3,2,1,0:T(8,128)(2,1)} reshape(bf16[16,2,65536]{2,1,0:T(2,128)(2,1)} %all-to-all-done.1) | data formatting | bytes 8388608
  887.8 17.2 %collective-permute-start.9 = (bf16[64,8,128]{0,2,1:T(8,128)(2,1)S(1)}, bf16[64,8,128]{0,2,1:T(8,128)(2,1)S(1)}, u32[]{:S(2)}, u32[]{:S(2)}) collective-permute-start(bf16[64,8,128]{0,2,1:T(8,128)(2,1)S(1)} %get-tuple-element.42), channel_id=1, source_target_pairs={{8,0},{16,8},{24,16},{32,24},{40,32},{48,40},{56,48},{64,56},{72,6... | collective-permute-start | bytes 393224 | tf_op jit(solution)/shard_map/ppermute | solution.py:17
  907.0 3.2 collective-permute-done.8
  911.6 4.0 collective-permute-start.10
  918.7 3.9 pad_maximum_fusion.7
  922.6 5.6 fusion.97
  940.9 4.7 collective-permute-start.12
  951.9 3.4 copy.160
  955.3 4.8 collective-permute-start.14
  960.2 3.3 copy.163
  967.0 3.1 copy.161
  970.9 3.9 copy.164
  974.8 7.9 maximum_maximum_fusion
  984.4 15.3 %fusion.25 = (bf16[64,24,8,128]{3,2,1,0:T(8,128)(2,1)S(1)}, bf16[64,24,8,128]{3,2,1,0:T(8,128)(2,1)S(1)}, bf16[64,24,8,128]{3,2,1,0:T(8,128)(2,1)S(1)}) fusion(bf16[64,16,128]{2,0,1:T(8,128)(2,1)S(1)} %copy.159, bf16[64,64,128]{2,0,1:T(8,128)(2,1)S(1)} %fusion.45, bf16[64,64,128]{2,0,1:T(8,128)(2,1)S(1)} %get-tuple-element.15, ...), kind=kLoop, calls=%fused_computation.46 | loop fusion | flops 34603008 | bytes 17301504
  (134 shorter events, 92.6 us)
Async XLA Ops:
  0.6 327.4 %copy-start.12 = (f32[2,64]{1,0:T(2,128)S(1)}, f32[2,64]{1,0:T(2,128)}, u32[]{:S(2)}) copy-start(f32[2,64]{1,0:T(2,128)} %param.14) | copy-start | bytes 1540
  308.9 19.2 %collective-permute-start.1 = (bf16[64,2,128]{2,0,1:T(8,128)(2,1)S(1)}, bf16[64,2,128]{2,0,1:T(8,128)(2,1)S(1)}, u32[]{:S(2)}, u32[]{:S(2)}) collective-permute-start(bf16[64,2,128]{2,0,1:T(8,128)(2,1)S(1)} %get-tuple-element.68), channel_id=1, source_target_pairs={{8,0},{16,8},{24,16},{32,24},{40,32},{48,40},{56,48},{64,56},{72,6... | collective-permute-start | bytes 98312 | tf_op jit(solution)/shard_map/ppermute | solution.py:17
  326.1 3.1 collective-permute-start
  329.3 6.1 copy-start.14
  331.3 4.3 collective-permute-start.2
  334.0 4.7 collective-permute-start.3
  344.5 8.5 copy-start.7
  355.6 7.2 collective-permute-start.5
  358.9 5.2 collective-permute-start.4
  366.8 5.0 collective-permute-start.6
  370.5 5.1 collective-permute-start.7
  382.5 9.4 copy-start.8
  394.2 4.4 copy-start
  424.2 55.8 %all-to-all-start = ((bf16[8,2,131072]{2,1,0:T(2,128)(2,1)}), bf16[8,2,131072]{2,1,0:T(2,128)(2,1)}, u32[]{:S(2)}, u32[]{:S(2)}) async-start(bf16[8,2,131072]{2,1,0:T(2,128)(2,1)} %reshape.289), calls=%async_computation | async-start | bytes 8388608 | tf_op jit(solution)/shard_map/all_to_all | solution.py:127
  518.2 4.9 copy-start.11
  518.2 350.4 %all-to-all-start.1 = ((bf16[16,2,65536]{2,1,0:T(2,128)(2,1)}), bf16[16,2,65536]{2,1,0:T(2,128)(2,1)}, u32[]{:S(2)}, u32[]{:S(2)}) async-start(bf16[16,2,65536]{2,1,0:T(2,128)(2,1)} %reshape.291), calls=%async_computation.1 | async-start | bytes 8388608 | tf_op jit(solution)/shard_map/all_to_all | solution.py:135
  885.7 21.3 %copy-start.9 = (bf16[3,64,384]{2,1,0:T(8,128)(2,1)S(1)}, bf16[3,64,384]{2,1,0:T(8,128)(2,1)}, u32[]{:S(2)}) copy-start(bf16[3,64,384]{2,1,0:T(8,128)(2,1)} %param.15) | copy-start | bytes 442372
  885.7 29.9 %copy-start.13 = (f32[2,64]{1,0:T(2,128)S(1)}, f32[2,64]{1,0:T(2,128)}, u32[]{:S(2)}) copy-start(f32[2,64]{1,0:T(2,128)} %param.17) | copy-start | bytes 1540
  887.8 19.2 %collective-permute-start.9 = (bf16[64,8,128]{0,2,1:T(8,128)(2,1)S(1)}, bf16[64,8,128]{0,2,1:T(8,128)(2,1)S(1)}, u32[]{:S(2)}, u32[]{:S(2)}) collective-permute-start(bf16[64,8,128]{0,2,1:T(8,128)(2,1)S(1)} %get-tuple-element.42), channel_id=1, source_target_pairs={{8,0},{16,8},{24,16},{32,24},{40,32},{48,40},{56,48},{64,56},{72,6... | collective-permute-start | bytes 393224 | tf_op jit(solution)/shard_map/ppermute | solution.py:17
  905.0 5.2 collective-permute-start.8
  910.3 6.6 collective-permute-start.11
  911.6 7.1 collective-permute-start.10
  928.2 1.6 copy-start.4
  929.8 1.6 copy-start.3
  931.4 1.6 copy-start.2
  938.8 8.7 collective-permute-start.13
  940.9 8.0 collective-permute-start.12
  951.9 13.0 %copy-start.1 = (f32[8192,64]{0,1:T(8,128)S(1)}, f32[8192,64]{0,1:T(8,128)}, u32[]{:S(2)}) copy-start(f32[8192,64]{0,1:T(8,128)} %copy-done) | copy-start | bytes 6291460
  955.3 11.6 %collective-permute-start.14 = (bf16[64,96,16]{1,2,0:T(8,128)(2,1)}, bf16[64,96,16]{1,2,0:T(8,128)(2,1)}, u32[]{:S(2)}, u32[]{:S(2)}) collective-permute-start(bf16[64,96,16]{1,2,0:T(8,128)(2,1)} %copy.160), channel_id=1, source_target_pairs={{0,1},{1,2},{2,3},{3,4},{4,5},{5,6},{6,7},{8,9},{9,10},{10,11},{11... | collective-permute-start | bytes 589832 | tf_op jit(solution)/shard_map/ppermute | solution.py:14
  963.4 7.4 collective-permute-start.15
  965.3 9.5 copy-start.6
  984.4 15.4 %copy-start.10 = (bf16[3,64,192]{2,1,0:T(8,128)(2,1)S(1)}, bf16[3,64,192]{2,1,0:T(8,128)(2,1)}, u32[]{:S(2)}) copy-start(bf16[3,64,192]{2,1,0:T(8,128)(2,1)} %param.16) | copy-start | bytes 221188
  (1 other events, 0.7 us)
where the time goes:
time: 1010 us; the launch traced here: 1000 us
  blocking collectives  649 us (64%)
  local copies, waits for them, and re-layouts  119 us (12%)
  starting transfers between devices  81.2 us (8%)
  other arithmetic  74.8 us (7%)
  waiting for transfers between devices  64.8 us (6%)
  matrix products  14.3 us (1%)
    all_gather x1, blocking collectives, per_device(): lax.all_gather(fine_feats, ('row', 'col'), axis=1, tiled=True)  343 us
    all_gather x1, blocking collectives, per_device(): lax.all_gather(coarse_feats, ('row', 'col'), axis=1, tiled=True)  306 us
    unnamed x36, local copies, waits for them, and re-layouts  54.5 us
    all_to_all x1, waiting for transfers between devices, per_device(): lax.all_to_all(outgoing, 'col', split_axis=0, concat_axis=0, tiled=True)  49.3 us
    ppermute x8, starting transfers between devices, with_halo(): lax.ppermute(lax.slice_in_dim(block, 0, width, axis=dim), axis, backward)  45.1 us
    unnamed x3, other arithmetic  33.3 us
    ppermute x8, starting transfers between devices, with_halo(): lax.ppermute(lax.slice_in_dim(block, block.shape[dim] - width, None, axis...  24.8 us
  transfers between devices with their start and end apart: 18, of which 11 were waited for; matrix products, arithmetic and copies ran while one was open for 2% of the time, Pallas kernels for 0%

commit v1 on v0

v1 whole, which is shorter than its diff:
```python
import functools

import jax
import jax.numpy as jnp
import numpy as np
from jax import lax
from jax.experimental import pallas as pl
from jax.experimental.pallas import tpu as pltpu
from jax.sharding import PartitionSpec as P

BF = jnp.bfloat16
F32 = jnp.float32
MESH = pl.DeviceIdType.MESH
VMEM_BYTES = 58 << 20
SIDE = 1024
ROWS, COLS = 16, 8
TR, TC = 64, 128

vmem = pl.BlockSpec(memory_space=pltpu.VMEM)
anywhere = pl.BlockSpec(memory_space=pl.ANY)


def lanes_of(shape):
    return lax.broadcasted_iota(jnp.int32, shape, len(shape) - 1)


def column_offsets(shape):
    lane = lanes_of(shape)
    return jnp.where(lane < 192, lane, lane - 256)


def shifted_stack(x, spacing, width):
    return jnp.concatenate(
        [
            pltpu.roll(x, spacing, 1)[:, :width],
            x[:, :width],
            pltpu.roll(x, 256 - spacing, 1)[:, :width],
        ],
        axis=0,
    )


def tap_products(w, source, target, count, group, spacing, width):
    def body(g, carry):
        stack = jnp.concatenate(
            [shifted_stack(source[g * group + t], spacing, width) for t in range(group)], axis=1
        )
        product = jnp.dot(w[...], stack, preferred_element_type=F32)
        for t in range(group):
            target[g * group + t, :, 0:width] = product[:, t * width : (t + 1) * width]
        return carry

    lax.fori_loop(0, count // group, body, 0)


def tap_sum(target, i, spacing, width):
    return (
        target[i, 0:64, 0:width]
        + target[i + spacing, 64:128, 0:width]
        + target[i + 2 * spacing, 128:192, 0:width]
    )


def prepare_kernel(prior, rows_out, left_out, right_out):
    for q in range(4):
        rows_out[16 * q : 16 * q + 16] = jnp.swapaxes(prior[:, 16 * q : 16 * q + 16, :], 0, 1)
    part = lanes_of((64, 128)) // 16

    def body(q, carry):
        left = rows_out[8 * q]
        right = pltpu.roll(left, 16, 1)
        for k in range(1, 8):
            x = rows_out[8 * q + k]
            left = jnp.where(part == k, pltpu.roll(x, 16 * k, 1), left)
            right = jnp.where(part == k, pltpu.roll(x, (16 * k + 16) % 128, 1), right)
        left_out[q] = left
        right_out[q] = right
        return carry

    lax.fori_loop(0, 8, body, 0)


def prepare(prior):
    return pl.pallas_call(
        prepare_kernel,
        out_shape=(
            jax.ShapeDtypeStruct((TR, 64, TC), BF),
            jax.ShapeDtypeStruct((8, 64, TC), BF),
            jax.ShapeDtypeStruct((8, 64, TC), BF),
        ),
        in_specs=[vmem],
        out_specs=(vmem, vmem, vmem),
        compiler_params=pltpu.CompilerParams(vmem_limit_bytes=VMEM_BYTES),
    )(prior)


def exchange_kernel(feats, tile, left, right, rows, rim_left, rim_right, gathered,
                    send, recv, send_a, recv_a, send_b, recv_b, own):
    r, c = lax.axis_index("row"), lax.axis_index("col")
    up, down = lax.rem(r + ROWS - 1, ROWS), lax.rem(r + 1, ROWS)
    west, east = lax.rem(c + COLS - 1, COLS), lax.rem(c + 1, COLS)
    barrier = pltpu.get_barrier_semaphore()
    for d in range(1, COLS):
        pl.semaphore_signal(
            barrier, 1, device_id=(r, lax.rem(c + d, COLS)), device_id_type=MESH
        )
    for d in range(1, ROWS):
        pl.semaphore_signal(
            barrier, 1, device_id=(lax.rem(r + d, ROWS), c), device_id_type=MESH
        )
    for a in (up, down):
        for b in (west, east):
            pl.semaphore_signal(barrier, 1, device_id=(a, b), device_id_type=MESH)
    pl.semaphore_wait(barrier, COLS - 1 + ROWS - 1 + 4)

    def copy(source, target, out_sem, in_sem, to):
        return pltpu.make_async_remote_copy(
            src_ref=source,
            dst_ref=target,
            send_sem=out_sem,
            recv_sem=in_sem,
            device_id=to,
            device_id_type=MESH,
        )

    place = r * COLS + c
    mine = pltpu.make_async_copy(feats, gathered.at[place], own)
    mine.start()
    first = [
        copy(feats, gathered.at[place], send_a.at[d], recv_a.at[d], (r, lax.rem(c + d, COLS)))
        for d in range(1, COLS)
    ]
    for x in first:
        x.start()
    rims = [
        (right, rim_left.at[pl.ds(2, 8)], (r, east)),
        (left, rim_right.at[pl.ds(2, 8)], (r, west)),
        (tile.at[pl.ds(54, 10)], rows.at[0], (down, c)),
        (tile.at[pl.ds(0, 10)], rows.at[1], (up, c)),
        (right.at[pl.ds(6, 2)], rim_left.at[pl.ds(0, 2)], (down, east)),
        (right.at[pl.ds(0, 2)], rim_left.at[pl.ds(10, 2)], (up, east)),
        (left.at[pl.ds(6, 2)], rim_right.at[pl.ds(0, 2)], (down, west)),
        (left.at[pl.ds(0, 2)], rim_right.at[pl.ds(10, 2)], (up, west)),
    ]
    rims = [copy(s, t, send.at[k], recv.at[k], to) for k, (s, t, to) in enumerate(rims)]
    for x in rims:
        x.start()
    mine.wait()
    for x in first:
        x.wait_recv()
    block = gathered.at[pl.ds(r * COLS, COLS)]
    second = [
        copy(block, block, send_b.at[d], recv_b.at[d], (lax.rem(r + d, ROWS), c))
        for d in range(1, ROWS)
    ]
    for x in second:
        x.start()
    for x in first:
        x.wait_send()
    for x in rims:
        x.wait()
    for x in second:
        x.wait()


def exchange(feats, tile, left, right):
    return pl.pallas_call(
        exchange_kernel,
        out_shape=(
            jax.ShapeDtypeStruct((2, 10, 64, TC), BF),
            jax.ShapeDtypeStruct((12, 64, TC), BF),
            jax.ShapeDtypeStruct((12, 64, TC), BF),
            jax.ShapeDtypeStruct((ROWS * COLS, 8, TC), BF),
        ),
        in_specs=[anywhere] * 4,
        out_specs=(anywhere,) * 4,
        scratch_shapes=[
            pltpu.SemaphoreType.DMA((8,)),
            pltpu.SemaphoreType.DMA((8,)),
            pltpu.SemaphoreType.DMA((COLS,)),
            pltpu.SemaphoreType.DMA((COLS,)),
            pltpu.SemaphoreType.DMA((ROWS,)),
            pltpu.SemaphoreType.DMA((ROWS,)),
            pltpu.SemaphoreType.DMA,
        ],
        compiler_params=pltpu.CompilerParams(collective_id=1, has_side_effects=True),
    )(feats, tile, left, right)


def chosen_bins(gathered, first, ring):
    lanes = 256 if ring else 128
    shape = (SIDE, lanes)
    wanted = first + (column_offsets(shape) if ring else lanes_of(shape))
    picked = lax.broadcasted_iota(jnp.int32, shape, 0) == wanted
    return lax.dot_general(
        gathered[...],
        jnp.where(picked, 1.0, 0.0).astype(BF),
        (((0,), (0,)), ((), ())),
        preferred_element_type=F32,
    )


def coarse_kernel(place, tile, rows, rim_left, rim_right, gathered, w1, w2, w3, bias,
                  map_out, pieces, edges, x, taps, hidden, fr, fc):
    r, c = place()
    row0, col0 = r * TR, c * TC
    fr[...] = chosen_bins(gathered, row0 - 16, False)[0:64]
    fc[...] = chosen_bins(gathered, col0, True)[0:64]
    cols = col0 + column_offsets((64, 256))
    in_cols = (cols >= 0) & (cols < SIDE)
    low_half = lanes_of((64, 128)) < 64

    def pair_row(q, k, at, body):
        shift = pltpu.roll(fr[...], lax.rem(256 - 8 * q, 128), 1)
        rim = jnp.where(
            low_half,
            pltpu.roll(rim_right[q], (128 - 16 * k) % 128, 1),
            pltpu.roll(rim_left[q], 112 - 16 * k, 1),
        )
        prior = jnp.concatenate([body, rim], axis=1).astype(F32)
        value = prior + (fc[...] + shift[:, k : k + 1])
        grow = row0 + 8 * q + k - 16
        inside = in_cols & (grow >= 0) & (grow < SIDE)
        x[at] = jnp.where(inside, value, 0.0).astype(BF)

    for k in range(10):
        row = k - 10
        pair_row((row + 16) // 8, row % 8, k, rows[0, k])
        row = 64 + k
        pair_row((row + 16) // 8, row % 8, 74 + k, rows[1, k])

    def own_rows(g, carry):
        for k in range(8):
            pair_row(g + 2, k, 8 * g + k + 10, tile[8 * g + k])
        return carry

    lax.fori_loop(0, 8, own_rows, 0)
    tap_products(w1, x, taps, 84, 12, 2, 256)

    def hidden_row(i, carry):
        for t in range(4):
            at = 4 * i + t
            grow = row0 + at - 8
            value = jnp.maximum(tap_sum(taps, at, 2, 256) + bias[0], 0.0)
            inside = in_cols & (grow >= 0) & (grow < SIDE)
            hidden[at] = jnp.where(inside, value, 0.0).astype(BF)
        return carry

    lax.fori_loop(0, 20, hidden_row, 0)
    tap_products(w2, hidden, taps, 80, 10, 4, 256)
    half_c, half_r = lax.rem(c, COLS // 2) * TC, lax.rem(r, ROWS // 2) * TR
    cols_q = half_c + column_offsets((64, 256))
    in_quarter = (cols_q >= 0) & (cols_q < SIDE // 2)

    def map_row(i, carry):
        for t in range(4):
            at = 4 * i + t
            qrow = half_r + at - 4
            value = jnp.maximum(tap_sum(taps, at, 4, 256) + bias[1], 0.0)
            inside = in_quarter & (qrow >= 0) & (qrow < SIDE // 2)
            x[at] = jnp.where(inside, value, 0.0).astype(BF)
        return carry

    lax.fori_loop(0, 18, map_row, 0)
    for q in range(4):
        map_out[:, 16 * q : 16 * q + 16, :] = jnp.swapaxes(
            x[4 + 16 * q : 20 + 16 * q, :, 0:128], 0, 1
        )
    tap_products(w3, x, taps, 72, 12, 4, 128)
    part = lanes_of((64, 128)) // 8

    def pack(g, carry):
        t, half = g // 2, lax.rem(g, 2)
        found = [None] * 4
        previous = None
        for k in range(16):
            v = tap_sum(taps, 16 * g + k, 4, 128).astype(BF)
            for n, start in enumerate((0, 56, 64, 120)):
                moved = pltpu.roll(v, (8 * k - start) % 128, 1)
                found[n] = moved if k == 0 else jnp.where(part == k, moved, found[n])
            if k % 2 == 0:
                previous = v
            else:
                at = 1 + 8 * half + k // 2
                pieces[t, at] = jnp.where(low_half, previous, pltpu.roll(v, 64, 1))
                pieces[2 + t, at] = jnp.where(low_half, pltpu.roll(previous, 64, 1), v)
        edges[t, half] = found[0]
        pieces[2 + t, 17 * half] = found[1]
        pieces[t, 17 * half] = found[2]
        edges[2 + t, half] = found[3]
        return carry

    lax.fori_loop(0, 4, pack, 0)


def mesh_place():
    return lax.axis_index("row"), lax.axis_index("col")


def coarse(place, tile, rows, rim_left, rim_right, gathered, w1, w2, w3, bias):
    return pl.pallas_call(
        functools.partial(coarse_kernel, place),
        out_shape=(
            jax.ShapeDtypeStruct((64, TR, TC), BF),
            jax.ShapeDtypeStruct((4, 18, 64, TC), BF),
            jax.ShapeDtypeStruct((4, 2, 64, TC), BF),
        ),
        in_specs=[vmem] * 9,
        out_specs=(vmem,) * 3,
        scratch_shapes=[
            pltpu.VMEM((84, 64, 256), BF),
            pltpu.VMEM((84, 192, 256), F32),
            pltpu.VMEM((80, 64, 256), BF),
            pltpu.VMEM((64, 128), F32),
            pltpu.VMEM((64, 256), F32),
        ],
        compiler_params=pltpu.CompilerParams(vmem_limit_bytes=VMEM_BYTES),
    )(tile, rows, rim_left, rim_right, gathered, w1, w2, w3, bias)


def move_kernel(half, pieces, edges, got, outer, top, top_outer, bottom, bottom_outer,
                send, recv, send_o, recv_o, send_n, recv_n, own, own_o):
    r, c = lax.axis_index("row"), lax.axis_index("col")
    base_r, base_c = half * (ROWS // 2), half * (COLS // 2)
    up, down = lax.rem(r + ROWS - 1, ROWS), lax.rem(r + 1, ROWS)
    tile_c = c // 2
    other_c = jnp.where(lax.rem(c, 2) == 0, lax.rem(tile_c + 3, 4), lax.rem(tile_c + 1, 4))
    from_r, from_c, from_o = base_r + r // 2, base_c + tile_c, base_c + other_c
    remote_main = (from_r != r) | (from_c != c)
    remote_outer = (from_r != r) | (from_o != c)
    is_source = (r >= base_r) & (r < base_r + ROWS // 2) & (c >= base_c) & (c < base_c + COLS // 2)
    local_r, local_c = r - base_r, c - base_c
    mains = [(2 * local_r + t, 2 * local_c + h) for h in range(2) for t in range(2)]
    outers = [(2 * local_r + t, 2 * lax.rem(local_c + 3, 4) + 1) for t in range(2)] + [
        (2 * local_r + t, 2 * lax.rem(local_c + 1, 4)) for t in range(2)
    ]

    def away(to):
        return (to[0] != r) | (to[1] != c)

    barrier = pltpu.get_barrier_semaphore()

    def greet(to):
        pl.semaphore_signal(barrier, 1, device_id=to, device_id_type=MESH)

    greet((up, c))
    greet((down, c))
    pl.when(remote_main)(lambda: greet((from_r, from_c)))
    pl.when(remote_outer)(lambda: greet((from_r, from_o)))
    for to in mains + outers:
        pl.when(is_source & away(to))(functools.partial(greet, to))
    peers = 2 + jnp.where(remote_main, 1, 0) + jnp.where(remote_outer, 1, 0)
    for to in mains + outers:
        peers = peers + jnp.where(is_source & away(to), 1, 0)
    pl.semaphore_wait(barrier, peers)

    def copy(source, target, out_sem, in_sem, to):
        return pltpu.make_async_remote_copy(
            src_ref=source,
            dst_ref=target,
            send_sem=out_sem,
            recv_sem=in_sem,
            device_id=to,
            device_id_type=MESH,
        )

    sends = [
        (copy(pieces.at[k], got, send.at[k], recv, to), to) for k, to in enumerate(mains)
    ] + [
        (copy(edges.at[k], outer, send_o.at[k], recv_o, to), to) for k, to in enumerate(outers)
    ]
    stay = [
        (pltpu.make_async_copy(pieces.at[k], got, own), to) for k, to in enumerate(mains)
    ] + [
        (pltpu.make_async_copy(edges.at[k], outer, own_o), to) for k, to in enumerate(outers)
    ]
    for (x, to), (y, _) in zip(sends, stay, strict=True):
        pl.when(is_source & away(to))(x.start)
        pl.when(is_source & jnp.logical_not(away(to)))(y.start)
    main_in = copy(pieces.at[0], got, send.at[0], recv, (up, c))
    outer_in = copy(edges.at[0], outer, send_o.at[0], recv_o, (up, c))
    pl.when(remote_main)(main_in.wait_recv)
    pl.when(jnp.logical_not(remote_main))(stay[0][0].wait)
    pl.when(remote_outer)(outer_in.wait_recv)
    pl.when(jnp.logical_not(remote_outer))(stay[4][0].wait)
    rims = [
        (got.at[pl.ds(13, 5)], top, (down, c)),
        (got.at[pl.ds(0, 5)], bottom, (up, c)),
        (outer.at[pl.ds(1, 1)], top_outer, (down, c)),
        (outer.at[pl.ds(0, 1)], bottom_outer, (up, c)),
    ]
    rims = [copy(s, t, send_n.at[k], recv_n.at[k], to) for k, (s, t, to) in enumerate(rims)]
    for x in rims:
        x.start()
    for x, to in sends:
        pl.when(is_source & away(to))(x.wait_send)
    for x in rims:
        x.wait()


def move(half, pieces, edges):
    return pl.pallas_call(
        functools.partial(move_kernel, half),
        out_shape=(
            jax.ShapeDtypeStruct((18, 64, TC), BF),
            jax.ShapeDtypeStruct((2, 64, TC), BF),
            jax.ShapeDtypeStruct((5, 64, TC), BF),
            jax.ShapeDtypeStruct((1, 64, TC), BF),
            jax.ShapeDtypeStruct((5, 64, TC), BF),
            jax.ShapeDtypeStruct((1, 64, TC), BF),
        ),
        in_specs=[anywhere] * 2,
        out_specs=(anywhere,) * 6,
        scratch_shapes=[
            pltpu.SemaphoreType.DMA((4,)),
            pltpu.SemaphoreType.DMA,
            pltpu.SemaphoreType.DMA((4,)),
            pltpu.SemaphoreType.DMA,
            pltpu.SemaphoreType.DMA((4,)),
            pltpu.SemaphoreType.DMA((4,)),
            pltpu.SemaphoreType.DMA,
            pltpu.SemaphoreType.DMA,
        ],
        compiler_params=pltpu.CompilerParams(collective_id=2 + half, has_side_effects=True),
    )(pieces, edges)


def spread_tables():
    lane = np.arange(128)
    source = np.arange(128)[:, None]
    main = np.stack([source == 64 * k + lane[None] // 2 for k in range(2)])
    rim = np.zeros((256, 16, 128), bool)
    for k in range(16):
        rim[:128, k] = (source == 8 * k + lane[None] // 2) & (lane[None] < 16)
        rim[128:, k] = (source == 8 * k + (lane[None] - 112) // 2) & (lane[None] >= 112)
    return main.astype(np.float32), rim.reshape(256, 2048).astype(np.float32)


def refine_kernel(place, got, outer, top, top_outer, bottom, bottom_outer, gathered,
                  wq, wp, w4, bias, main_table, rim_table,
                  out, wide, hidden, taps, row_terms, row_part):
    r, c = place()
    row0, col0 = r * TR, c * TC
    fc = chosen_bins(gathered, col0, True)[64:128].astype(BF)
    q = jnp.dot(wq[...], shifted_stack(fc, 8, 256), preferred_element_type=F32)
    base = q[64:128] + bias[0]
    row_terms[0] = base + q[0:64] + q[128:192]
    row_terms[1] = base + q[128:192]
    row_terms[2] = base + q[0:64]
    fr = chosen_bins(gathered, row0 - 24, False)[64:128].astype(BF)
    stack = jnp.concatenate([pltpu.roll(fr, 8, 1), fr, pltpu.roll(fr, 120, 1)], axis=0)
    p = jnp.dot(wp[...], stack, preferred_element_type=F32)
    row_part[0] = p[0:64] + p[64:128] + p[128:192]
    row_part[1] = p[64:128] + jnp.where(c == 0, p[128:192], p[0:64])
    cols = col0 + column_offsets((64, 256))
    in_cols = (cols >= 0) & (cols < SIDE)
    at_edge = (cols < 8) | (cols >= SIDE - 8)

    def spread_main(source, first, count, at):
        for k in range(2):
            value = jnp.dot(
                source[first : first + count].reshape(count * 64, 128),
                main_table[k],
                preferred_element_type=F32,
            )
            wide[at : at + count, k, :, 0:128] = value.reshape(count, 64, 128).astype(BF)

    spread_main(top, 0, 4, 0)
    spread_main(got, 1, 16, 4)
    spread_main(bottom, 1, 4, 20)
    inner_right = lax.rem(c, 2) == 0

    def spread_rim(inside, outside, low, high, first):
        both = jnp.concatenate(
            [
                jnp.where(inner_right, inside, outside),
                jnp.where(inner_right, outside, inside),
            ],
            axis=1,
        )
        value = jnp.dot(
            both, rim_table[:, 128 * low : 128 * high], preferred_element_type=F32
        ).astype(BF)
        for k in range(high - low):
            row = first + k
            wide[row // 2, row % 2, :, 128:256] = value[:, 128 * k : 128 * k + 128]

    spread_rim(top[4], top_outer[0], 8, 16, 0)
    spread_rim(got[0], outer[0], 0, 16, 8)
    spread_rim(got[17], outer[1], 0, 16, 24)
    spread_rim(bottom[0], bottom_outer[0], 0, 8, 40)

    def hidden_rows(g, carry):
        grow0 = row0 + 8 * g - 16
        inside = in_cols & (grow0 >= 0) & (grow0 < SIDE)
        variant = jnp.where(grow0 == 0, 1, jnp.where(grow0 == SIDE - 8, 2, 0))
        shift = lax.rem(256 - 8 * g - 8, 128)
        everywhere = pltpu.roll(row_part[0], shift, 1)
        edge = pltpu.roll(row_part[1], shift, 1)
        terms = row_terms[variant]
        for k in range(8):
            row = jnp.where(at_edge, edge[:, k : k + 1], everywhere[:, k : k + 1])
            value = wide[2 * g + k // 4, (k // 2) % 2].astype(F32) + (terms + row)
            hidden[8 * g + k] = jnp.where(inside, jnp.maximum(value, 0.0), 0.0).astype(BF)
        return carry

    lax.fori_loop(0, 12, hidden_rows, 0)
    tap_products(w4, hidden, taps, 96, 12, 16, 128)

    for g in range(4):
        value = jnp.stack(
            [
                jnp.maximum(tap_sum(taps, 16 * g + k, 16, 128) + bias[1, :, 0:128], 0.0).astype(BF)
                for k in range(16)
            ]
        )
        out[:, 16 * g : 16 * g + 16, :] = jnp.swapaxes(value, 0, 1)


def refine(place, got, outer, top, top_outer, bottom, bottom_outer, gathered, wq, wp, w4, bias):
    main_table, rim_table = spread_tables()
    return pl.pallas_call(
        functools.partial(refine_kernel, place),
        out_shape=jax.ShapeDtypeStruct((64, TR, TC), BF),
        in_specs=[vmem] * 13,
        out_specs=vmem,
        scratch_shapes=[
            pltpu.VMEM((24, 2, 64, 256), BF),
            pltpu.VMEM((96, 64, 256), BF),
            pltpu.VMEM((96, 192, 128), F32),
            pltpu.VMEM((3, 64, 256), F32),
            pltpu.VMEM((2, 64, 128), F32),
        ],
        compiler_params=pltpu.CompilerParams(vmem_limit_bytes=VMEM_BYTES),
    )(got, outer, top, top_outer, bottom, bottom_outer, gathered, wq, wp, w4, bias,
      jnp.asarray(main_table, BF), jnp.asarray(rim_table, BF))


def weight_forms(coarse_weights, coarse_bias, refine_first, refine_second, refine_bias):
    w1 = coarse_weights[0].reshape(192, 192)
    w2 = coarse_weights[1].reshape(192, 192)
    first = refine_first.reshape(3, 64, 3, 128)
    w3 = first[..., :64].reshape(192, 192)
    fine = first[..., 64:]
    wq = fine.reshape(192, 192)
    wp = fine.transpose(2, 1, 0, 3).reshape(192, 192)
    w4 = refine_second.reshape(192, 192)
    b12 = jnp.broadcast_to(coarse_bias[:, :, None], (2, 64, 256))
    b34 = jnp.broadcast_to(refine_bias[:, :, None], (2, 64, 256))
    return w1, w2, w3, wq, wp, w4, b12, b34


def per_device(coarse_feats, fine_feats, pair_prior, zoom_start, coarse_weights, coarse_bias,
               refine_first, refine_second, refine_bias):
    w1, w2, w3, wq, wp, w4, b12, b34 = weight_forms(
        coarse_weights, coarse_bias, refine_first, refine_second, refine_bias
    )
    feats = jnp.concatenate([coarse_feats, fine_feats], axis=0).T
    tile, left, right = prepare(pair_prior)
    rows, rim_left, rim_right, gathered = exchange(feats, tile, left, right)
    gathered = gathered.reshape(SIDE, 128)
    coarse_map, pieces, edges = coarse(
        mesh_place, tile, rows, rim_left, rim_right, gathered, w1, w2, w3, b12
    )
    moved = lax.cond(
        zoom_start[0] == 0,
        functools.partial(move, 0),
        functools.partial(move, 1),
        pieces,
        edges,
    )
    refined = refine(mesh_place, *moved, gathered, wq, wp, w4, b34)
    return coarse_map, refined


def solution(mesh):
    return jax.shard_map(
        per_device,
        mesh=mesh,
        in_specs=(
            P(None, ("row", "col")),
            P(None, ("row", "col")),
            P(None, "row", "col"),
            P(),
            P(),
            P(),
            P(),
            P(),
            P(),
        ),
        out_specs=(P(None, "row", "col"), P(None, "row", "col")),
        check_vma=False,
    )
```

time: 1010 us -> 111 us (0.11)
  blocking collectives: 649 us -> 0 us
  local copies, waits for them, and re-layouts: 119 us -> 8.17 us
  Pallas kernels: 0 us -> 99.5 us
  starting transfers between devices: 81.2 us -> 0 us
  other arithmetic: 74.8 us -> 1.35 us
  waiting for transfers between devices: 64.8 us -> 0 us
  matrix products: 14.3 us -> 0 us
    all_gather x2 -> x0, blocking collectives: 649 us -> none  [the longest x1 343 us: per_device(): lax.all_gather(fine_feats, ('row', 'col'), axis=1, tiled=True)]
    pallas_call x0 -> x5, Pallas kernels: none -> 99.5 us  [the longest x1 39.7 us: move(): pl.pallas_call(functools.partial(move_kernel, half), out_shape=(jax.Shape...]
    ppermute x16 -> x0, starting transfers between devices: 69.9 us -> none  [the longest x8 45.1 us: with_halo(): lax.ppermute(lax.slice_in_dim(block, 0, width, axis=dim), axis, backward)]
    unnamed x36 -> x0, local copies, waits for them, and re-layouts: 54.5 us -> none
    all_to_all x2 -> x0, waiting for transfers between devices: 49.3 us -> none  [the longest x1 49.3 us: per_device(): lax.all_to_all(outgoing, 'col', split_axis=0, concat_axis=0, tiled=True)]
    unnamed x3 -> x0, other arithmetic: 33.3 us -> none
    slice x21 -> x1, local copies, waits for them, and re-layouts: 27.4 us -> 1.64 us  [weight_forms(): w2 = coarse_weights[1].reshape(192, 192)]
    concatenate x7 -> x0, other arithmetic: 16.8 us -> none  [the longest x6 12.9 us: with_halo(): block = jnp.concatenate([low, block, high], axis=dim)]
  transfers between devices with their start and end apart: 18 -> 0, of which waited for: 11 -> 0; matrix products, arithmetic and copies ran while one was open for 2% -> 0% of each run, Pallas kernels for 0% -> 0%
where the time goes in v1:
time: 111 us; the launch traced here: 110 us
  Pallas kernels  99.5 us (90%)
  local copies, waits for them, and re-layouts  8.17 us (7%)
  other arithmetic  1.35 us (1%)
  between operations  1.32 us (1%)
    pallas_call x1, Pallas kernels, move(): pl.pallas_call(functools.partial(move_kernel, half), out_shape=(jax.Shape...  39.7 us
    pallas_call x1, Pallas kernels, coarse(): pl.pallas_call(functools.partial(coarse_kernel, place), out_shape=(jax.Sh...  22.4 us
    pallas_call x1, Pallas kernels, exchange(): pl.pallas_call(exchange_kernel, out_shape=(jax.ShapeDtypeStruct((2, 10, 6...  21.5 us
    pallas_call x1, Pallas kernels, refine(): pl.pallas_call(functools.partial(refine_kernel, place), out_shape=jax.Sha...  12.3 us
    pallas_call x1, Pallas kernels, prepare(): pl.pallas_call(prepare_kernel, out_shape=(jax.ShapeDtypeStruct((TR, 64, T...  3.62 us

profile of v1, /device:TPU:1, one launch (start us, length us, event | category | flops | bytes accessed | tf_op | source)
XLA Modules:
  0.0 110.3 jit_solution(2373117939528421506)
XLA Ops:
  1.3 1.3 %maximum_bitcast_fusion.feats = bf16[8,128]{1,0:T(8,128)(2,1)} fusion(bf16[64,8]{0,1:T(8,128)(2,1)} %param.14, bf16[64,8]{0,1:T(8,128)(2,1)} %param.13), kind=kLoop, calls=%fused_computation | loop fusion | flops 4096 | bytes 4096 | tf_op jit(solution)/shard_map/transpose | solution.py:558
  2.6 1.4 %broadcast_in_dim.4.bias = f32[2,64,256]{2,1,0:T(8,128)} broadcast(f32[2,64]{1,0:T(2,128)} %param.18), dimensions={0,1} | broadcast | bytes 131584 | tf_op jit(solution)/shard_map/broadcast_in_dim | solution.py:548
  4.0 1.4 %broadcast_in_dim.5.bias = f32[2,64,256]{2,1,0:T(8,128)} broadcast(f32[2,64]{1,0:T(2,128)} %param.21), dimensions={0,1} | broadcast | bytes 131584 | tf_op jit(solution)/shard_map/broadcast_in_dim | solution.py:549
  5.4 1.0 reshape.29
  6.4 1.6 %fusion = (bf16[1,3,64,192]{3,2,1,0:T(8,128)(2,1)}, bf16[1,3,64,192]{3,2,1,0:T(8,128)(2,1)}) fusion(bf16[2,3,64,192]{3,2,1,0:T(8,128)(2,1)} %param.17), kind=kLoop, calls=%fused_computation.2 | loop fusion | bytes 294912 | tf_op jit(solution)/shard_map/slice | solution.py:541
  8.0 0.2 slice_bitcast_fusion
  8.3 0.2 copy.15
  8.4 0.8 reshape.32.wp
  9.2 0.8 reshape.31.wq
  10.0 0.8 reshape.30.w3
  10.8 3.6 %shard_map.122 = (bf16[64,64,128]{2,1,0:T(8,128)(2,1)}, bf16[8,64,128]{2,1,0:T(8,128)(2,1)}, bf16[8,64,128]{2,1,0:T(8,128)(2,1)}) custom-call(bf16[64,64,128]{2,1,0:T(8,128)(2,1)} %prior.1), custom_call_target="tpu_custom_call" | custom-call | tf_op jit(solution)/shard_map/pallas_call | solution.py:84
  14.4 21.5 %shard_map.123 = (bf16[2,10,64,128]{3,2,1,0:T(8,128)(2,1)}, bf16[12,64,128]{2,1,0:T(8,128)(2,1)}, bf16[12,64,128]{2,1,0:T(8,128)(2,1)}, bf16[128,8,128]{2,1,0:T(8,128)(2,1)}) custom-call(bf16[8,128]{1,0:T(8,128)(2,1)} %maximum_bitcast_fusion.feats, bf16[64,64,128]{2,1,0:T(8,128)(2,1)} %get-tuple-element.30.tile, bf16[8,64,128]{2,1,0:T(8,128)(2,1)} %get-tuple-element.31.left, ...), custom_call_target="tpu_custom_call" | custom-call | tf_op jit(solution)/shard_map/pallas_call | solution.py:167
  36.0 22.4 %shard_map.124 = (bf16[64,64,128]{2,1,0:T(8,128)(2,1)}, bf16[4,18,64,128]{3,2,1,0:T(8,128)(2,1)S(1)}, bf16[4,2,64,128]{3,2,1,0:T(8,128)(2,1)S(1)}) custom-call(bf16[64,64,128]{2,1,0:T(8,128)(2,1)} %get-tuple-element.30.tile, bf16[2,10,64,128]{3,2,1,0:T(8,128)(2,1)} %get-tuple-element.33.rows, bf16[12,64,128]{2,1,0:T(8,128)(2,1)} %get-tuple-element.34.rim_left, ...), custom_call_target="tpu_custom_call" | custom-call | tf_op jit(solution)/shard_map/pallas_call | solution.py:301
  58.3 39.7 %conditional.1 = ((bf16[18,64,128]{2,1,0:T(8,128)(2,1)S(1)}, bf16[2,64,128]{2,1,0:T(8,128)(2,1)S(1)}, bf16[5,64,128]{2,1,0:T(8,128)(2,1)S(1)}, bf16[1,64,128]{2,...) conditional(s32[]{:T(128)} %bitcast.4, ...), branch_computations={%region_0.0_spmd, %region_1.0_spmd} | conditional | bytes 8 | solution.py:565
  58.3 39.7 %branch_0_fun.1 = (bf16[18,64,128]{2,1,0:T(8,128)(2,1)S(1)}, bf16[2,64,128]{2,1,0:T(8,128)(2,1)S(1)}, bf16[5,64,128]{2,1,0:T(8,128)(2,1)S(1)}, bf16[1,64,128]{2,...) custom-call(bf16[4,18,64,128]{3,2,1,0:T(8,128)(2,1)S(1)} %get-tuple-element.8.pieces, ...), custom_call_target="tpu_custom_call" | custom-call | tf_op jit(solution)/shard_map/cond/branch_0_fun/pallas_call | solution.py:402
  98.1 12.3 %shard_map.125 = bf16[64,64,128]{2,1,0:T(8,128)(2,1)} custom-call(bf16[18,64,128]{2,1,0:T(8,128)(2,1)S(1)} %get-tuple-element.40.got, bf16[2,64,128]{2,1,0:T(8,128)(2,1)S(1)} %get-tuple-element.41.outer, bf16[5,64,128]{2,1,0:T(8,128)(2,1)S(1)} %get-tuple-element.42.top, bf16[1,64,128]{2,1,0:T(8,128)(2,1)S(1)} %get-tuple-element.43.top_outer, ...), custom_call_target="tpu_custom_call" | custom-call | tf_op jit(solution)/shard_map/pallas_call | solution.py:522

commit v2 on v1

v2 whole, which is shorter than its diff:
```python
import functools

import jax
import jax.numpy as jnp
import numpy as np
from jax import lax
from jax.experimental import pallas as pl
from jax.experimental.pallas import tpu as pltpu
from jax.sharding import PartitionSpec as P

BF = jnp.bfloat16
F32 = jnp.float32
MESH = pl.DeviceIdType.MESH
VMEM_BYTES = 58 << 20
SIDE = 1024
ROWS, COLS = 16, 8
TR, TC = 64, 128

vmem = pl.BlockSpec(memory_space=pltpu.VMEM)
anywhere = pl.BlockSpec(memory_space=pl.ANY)


def lanes_of(shape):
    return lax.broadcasted_iota(jnp.int32, shape, len(shape) - 1)


def column_offsets(shape):
    lane = lanes_of(shape)
    return jnp.where(lane < 192, lane, lane - 256)


def shifted_stack(x, spacing, width):
    return jnp.concatenate(
        [
            pltpu.roll(x, spacing, 1)[:, :width],
            x[:, :width],
            pltpu.roll(x, 256 - spacing, 1)[:, :width],
        ],
        axis=0,
    )


def tap_products(w, source, first, target, into, count, group, spacing, width):
    for g in range(count // group):
        base = first + g * group
        stack = jnp.concatenate(
            [shifted_stack(source[base + t], spacing, width) for t in range(group)], axis=1
        )
        product = jnp.dot(w, stack, preferred_element_type=F32)
        for t in range(group):
            target[into + g * group + t] = product[:, t * width : (t + 1) * width]


def carry_taps(target, spacing):
    last = target.shape[0] - 2 * spacing
    for t in range(2 * spacing):
        target[t, 0:64] = target[last + t, 0:64]
        if t >= spacing:
            target[t, 64:128] = target[last + t, 64:128]


def tap_sum(target, i, spacing, width):
    return (
        target[i, 0:64, 0:width]
        + target[i + spacing, 64:128, 0:width]
        + target[i + 2 * spacing, 128:192, 0:width]
    )


def bias_columns(bias, layer, width):
    row = jnp.broadcast_to(bias[layer : layer + 1, :], (128, 64))
    column = jnp.transpose(row)
    return column if width == 128 else jnp.concatenate([column, column], axis=1)


def halves_joined(a, b, c, upper):
    low = lanes_of(a.shape) < 64
    if upper:
        first = jnp.where(low, pltpu.roll(a, 64, 1), b)
        return jnp.concatenate([first, pltpu.roll(c, 64, 1)[:, :64]], axis=1)
    first = jnp.where(low, a, pltpu.roll(b, 64, 1))
    return jnp.concatenate([first, c[:, :64]], axis=1)


def gather_kernel(coarse_feats, fine_feats, prior, tile, rows, rim_left, rim_right, gathered,
                  feats, left, right, send, recv, send_a, recv_a, send_b, recv_b, own):
    r, c = lax.axis_index("row"), lax.axis_index("col")
    up, down = lax.rem(r + ROWS - 1, ROWS), lax.rem(r + 1, ROWS)
    west, east = lax.rem(c + COLS - 1, COLS), lax.rem(c + 1, COLS)
    has_up, has_down, has_west, has_east = r > 0, r < ROWS - 1, c > 0, c < COLS - 1
    barrier = pltpu.get_barrier_semaphore()

    def greet(to):
        pl.semaphore_signal(barrier, 1, device_id=to, device_id_type=MESH)

    for d in range(1, COLS):
        greet((r, lax.rem(c + d, COLS)))
    for d in range(1, ROWS):
        greet((lax.rem(r + d, ROWS), c))
    peers = COLS - 1 + ROWS - 1
    for a, has_a in ((up, has_up), (down, has_down)):
        for b, has_b in ((west, has_west), (east, has_east)):
            pl.when(has_a & has_b)(functools.partial(greet, (a, b)))
            peers = peers + jnp.where(has_a & has_b, 1, 0)

    both = jnp.concatenate([coarse_feats[...], fine_feats[...]], axis=0).astype(F32)
    feats[...] = jnp.transpose(both).astype(BF)
    for q in range(4):
        tile[16 * q : 16 * q + 16] = jnp.swapaxes(prior[:, 16 * q : 16 * q + 16, :], 0, 1)
    part = lanes_of((64, 128)) // 16

    def pack(q, carry):
        low = tile[8 * q]
        high = pltpu.roll(low, 16, 1)
        for k in range(1, 8):
            x = tile[8 * q + k]
            low = jnp.where(part == k, pltpu.roll(x, 16 * k, 1), low)
            high = jnp.where(part == k, pltpu.roll(x, (16 * k + 16) % 128, 1), high)
        left[q] = low
        right[q] = high
        return carry

    def copy(source, target, out_sem, in_sem, to):
        return pltpu.make_async_remote_copy(
            src_ref=source,
            dst_ref=target,
            send_sem=out_sem,
            recv_sem=in_sem,
            device_id=to,
            device_id_type=MESH,
        )

    pl.semaphore_wait(barrier, peers)
    place = r * COLS + c
    mine = pltpu.make_async_copy(feats, gathered.at[place], own)
    mine.start()
    first = [
        copy(feats, gathered.at[place], send_a.at[d], recv_a.at[d], (r, lax.rem(c + d, COLS)))
        for d in range(1, COLS)
    ]
    for x in first:
        x.start()
    lax.fori_loop(0, 8, pack, 0)
    rims = [
        (right, rim_left.at[pl.ds(2, 8)], (r, east), has_east, has_west),
        (left, rim_right.at[pl.ds(2, 8)], (r, west), has_west, has_east),
        (tile.at[pl.ds(54, 10)], rows.at[0], (down, c), has_down, has_up),
        (tile.at[pl.ds(0, 10)], rows.at[1], (up, c), has_up, has_down),
        (right.at[pl.ds(6, 2)], rim_left.at[pl.ds(0, 2)], (down, east),
         has_down & has_east, has_up & has_west),
        (right.at[pl.ds(0, 2)], rim_left.at[pl.ds(10, 2)], (up, east),
         has_up & has_east, has_down & has_west),
        (left.at[pl.ds(6, 2)], rim_right.at[pl.ds(0, 2)], (down, west),
         has_down & has_west, has_up & has_east),
        (left.at[pl.ds(0, 2)], rim_right.at[pl.ds(10, 2)], (up, west),
         has_up & has_west, has_down & has_east),
    ]
    rims = [
        (copy(s, t, send.at[k], recv.at[k], to), out, into)
        for k, (s, t, to, out, into) in enumerate(rims)
    ]
    for x, out, _ in rims:
        pl.when(out)(x.start)
    mine.wait()
    for x in first:
        x.wait_recv()
    block = gathered.at[pl.ds(r * COLS, COLS)]
    second = [
        copy(block, block, send_b.at[d], recv_b.at[d], (lax.rem(r + d, ROWS), c))
        for d in range(1, ROWS)
    ]
    for x in second:
        x.start()
    for x in first:
        x.wait_send()
    for x, out, into in rims:
        pl.when(out)(x.wait_send)
        pl.when(into)(x.wait_recv)
    for x in second:
        x.wait()


def gather(coarse_feats, fine_feats, prior):
    return pl.pallas_call(
        gather_kernel,
        out_shape=(
            jax.ShapeDtypeStruct((TR, 64, TC), BF),
            jax.ShapeDtypeStruct((2, 10, 64, TC), BF),
            jax.ShapeDtypeStruct((12, 64, TC), BF),
            jax.ShapeDtypeStruct((12, 64, TC), BF),
            jax.ShapeDtypeStruct((ROWS * COLS, 8, TC), BF),
        ),
        in_specs=[vmem] * 3,
        out_specs=(vmem,) + (anywhere,) * 4,
        scratch_shapes=[
            pltpu.VMEM((8, TC), BF),
            pltpu.VMEM((8, 64, TC), BF),
            pltpu.VMEM((8, 64, TC), BF),
            pltpu.SemaphoreType.DMA((8,)),
            pltpu.SemaphoreType.DMA((8,)),
            pltpu.SemaphoreType.DMA((COLS,)),
            pltpu.SemaphoreType.DMA((COLS,)),
            pltpu.SemaphoreType.DMA((ROWS,)),
            pltpu.SemaphoreType.DMA((ROWS,)),
            pltpu.SemaphoreType.DMA,
        ],
        compiler_params=pltpu.CompilerParams(
            collective_id=1, has_side_effects=True, vmem_limit_bytes=VMEM_BYTES
        ),
    )(coarse_feats, fine_feats, prior)


def chosen_bins(gathered, first, ring):
    lanes = 256 if ring else 128
    shape = (SIDE, lanes)
    wanted = first + (column_offsets(shape) if ring else lanes_of(shape))
    picked = lax.broadcasted_iota(jnp.int32, shape, 0) == wanted
    return lax.dot_general(
        gathered[...],
        jnp.where(picked, 1.0, 0.0).astype(BF),
        (((0,), (0,)), ((), ())),
        preferred_element_type=F32,
    )


def coarse_kernel(half, tile, rows, rim_left, rim_right, gathered, weights, first_refine, biases,
                  map_out, got, outer, top, top_outer, bottom, bottom_outer,
                  x, taps1, hidden, taps2, fields, taps3, w3, bias, fr, fc, pieces, edges,
                  send, recv, send_o, recv_o, send_n, recv_n, own, own_o):
    r, c = lax.axis_index("row"), lax.axis_index("col")
    base_r, base_c = half * (ROWS // 2), half * (COLS // 2)
    up, down = lax.rem(r + ROWS - 1, ROWS), lax.rem(r + 1, ROWS)
    tile_c = c // 2
    other_c = jnp.where(lax.rem(c, 2) == 0, lax.rem(tile_c + 3, 4), lax.rem(tile_c + 1, 4))
    from_r, from_c, from_o = base_r + r // 2, base_c + tile_c, base_c + other_c
    remote_main = (from_r != r) | (from_c != c)
    remote_outer = (from_r != r) | (from_o != c)
    is_source = (r >= base_r) & (r < base_r + ROWS // 2) & (c >= base_c) & (c < base_c + COLS // 2)
    local_r, local_c = r - base_r, c - base_c

    def main_to(t, h):
        return 2 * local_r + t, 2 * local_c + h

    def outer_to(t, side):
        if side == 0:
            return 2 * local_r + t, 2 * lax.rem(local_c + 3, 4) + 1
        return 2 * local_r + t, 2 * lax.rem(local_c + 1, 4)

    def away(to):
        return (to[0] != r) | (to[1] != c)

    barrier = pltpu.get_barrier_semaphore()

    def greet(to):
        pl.semaphore_signal(barrier, 1, device_id=to, device_id_type=MESH)

    greet((up, c))
    greet((down, c))
    pl.when(remote_main)(lambda: greet((from_r, from_c)))
    pl.when(remote_outer)(lambda: greet((from_r, from_o)))
    peers = 2 + jnp.where(remote_main, 1, 0) + jnp.where(remote_outer, 1, 0)
    for t in range(2):
        for k in range(2):
            for to in (main_to(t, k), outer_to(t, k)):
                pl.when(is_source & away(to))(functools.partial(greet, to))
                peers = peers + jnp.where(is_source & away(to), 1, 0)

    def copy(source, target, out_sem, in_sem, to):
        return pltpu.make_async_remote_copy(
            src_ref=source,
            dst_ref=target,
            send_sem=out_sem,
            recv_sem=in_sem,
            device_id=to,
            device_id_type=MESH,
        )

    def transfers(j):
        t, q = j // 2, lax.rem(j, 2)
        found = []
        for k in range(2):
            to = main_to(t, k)
            s, d = pieces.at[k, t, pl.ds(9 * q, 9)], got.at[pl.ds(9 * q, 9)]
            found.append(
                (copy(s, d, send.at[2 * j + k], recv.at[q], to),
                 pltpu.make_async_copy(s, d, own.at[q]), to)
            )
            to = outer_to(t, k)
            s, d = edges.at[k, t, pl.ds(q, 1)], outer.at[pl.ds(q, 1)]
            found.append(
                (copy(s, d, send_o.at[2 * j + k], recv_o.at[q], to),
                 pltpu.make_async_copy(s, d, own_o.at[q]), to)
            )
        return found

    w1 = weights[0].reshape(192, 192)
    w2 = weights[1].reshape(192, 192)
    joined = first_refine[...].reshape(192, 384)
    w3[...] = halves_joined(joined[:, 0:128], joined[:, 128:256], joined[:, 256:384], False)
    bias[0] = bias_columns(biases, 0, 256)
    bias[1] = bias_columns(biases, 1, 256)
    row0, col0 = r * TR, c * TC
    fr[...] = chosen_bins(gathered, row0 - 16, False)[0:64]
    fc[...] = chosen_bins(gathered, col0, True)[0:64]
    cols = col0 + column_offsets((64, 256))
    in_cols = (cols >= 0) & (cols < SIDE)
    half_c, half_r = lax.rem(c, COLS // 2) * TC, lax.rem(r, ROWS // 2) * TR
    cols_q = half_c + column_offsets((64, 256))
    in_quarter = (cols_q >= 0) & (cols_q < SIDE // 2)
    low_half = lanes_of((64, 128)) < 64
    part = lanes_of((64, 128)) // 8

    def pair_row(q, k, at, body, shift):
        rim = jnp.where(
            low_half,
            pltpu.roll(rim_right[q], (128 - 16 * k) % 128, 1),
            pltpu.roll(rim_left[q], 112 - 16 * k, 1),
        )
        prior = jnp.concatenate([body, rim], axis=1).astype(F32)
        value = prior + (fc[...] + shift[:, k : k + 1])
        grow = row0 + 8 * q + k - 16
        inside = in_cols & (grow >= 0) & (grow < SIDE)
        x[at] = jnp.where(inside, value, 0.0).astype(BF)

    def features_at(q):
        return pltpu.roll(fr[...], lax.rem(256 - 8 * q, 128), 1)

    def rim_rows(side):
        for k in range(10):
            row = 64 + k if side else k - 10
            q = (row + 16) // 8
            pair_row(q, row % 8, row + 10, rows[side, k], features_at(q))

    def own_rows(g):
        shift = features_at(g + 2)
        for k in range(8):
            pair_row(g + 2, k, 8 * g + k + 10, tile[8 * g + k], shift)

    def hidden_rows(first, taken, count):
        for t in range(count):
            at = first + t
            grow = row0 + at - 8
            value = jnp.maximum(tap_sum(taps1, taken + t, 2, 256) + bias[0], 0.0)
            inside = in_cols & (grow >= 0) & (grow < SIDE)
            hidden[at] = jnp.where(inside, value, 0.0).astype(BF)

    def field_rows(first, taken, count):
        for t in range(count):
            at = first + t
            qrow = half_r + at - 4
            value = jnp.maximum(tap_sum(taps2, taken + t, 4, 256) + bias[1], 0.0)
            inside = in_quarter & (qrow >= 0) & (qrow < SIDE // 2)
            fields[at] = jnp.where(inside, value, 0.0).astype(BF)

    def pack(j):
        t, q = j // 2, lax.rem(j, 2)
        found = [None] * 4
        previous = None
        for k in range(16):
            v = tap_sum(taps3, k, 4, 128).astype(BF)
            for n, start in enumerate((0, 56, 64, 120)):
                moved = pltpu.roll(v, (8 * k - start) % 128, 1)
                found[n] = moved if k == 0 else jnp.where(part == k, moved, found[n])
            if k % 2 == 0:
                previous = v
            else:
                at = 1 + 8 * q + k // 2
                pieces[0, t, at] = jnp.where(low_half, previous, pltpu.roll(v, 64, 1))
                pieces[1, t, at] = jnp.where(low_half, pltpu.roll(previous, 64, 1), v)
        edges[0, t, q] = found[0]
        pieces[1, t, 17 * q] = found[1]
        pieces[0, t, 17 * q] = found[2]
        edges[1, t, q] = found[3]

    rim_rows(0)

    def early_rows(g, carry):
        own_rows(g)
        return carry

    lax.fori_loop(0, 4, early_rows, 0)
    tap_products(w1, x, 0, taps1, 0, 20, 10, 2, 256)
    hidden_rows(0, 0, 16)
    tap_products(w2, hidden, 0, taps2, 8, 16, 8, 4, 256)
    field_rows(0, 8, 8)
    tap_products(w3[...], fields, 0, taps3, 16, 8, 8, 4, 128)
    pl.semaphore_wait(barrier, peers)

    def chunk(j, carry):
        @pl.when((j == 1) | (j == 2))
        def _():
            own_rows(2 * j + 2)
            own_rows(2 * j + 3)

        pl.when(j == 3)(lambda: rim_rows(1))
        carry_taps(taps1, 2)
        carry_taps(taps2, 4)
        carry_taps(taps3, 4)
        tap_products(w1, x, 20 + 16 * j, taps1, 4, 16, 8, 2, 256)
        hidden_rows(16 + 16 * j, 0, 16)
        tap_products(w2, hidden, 16 + 16 * j, taps2, 8, 16, 8, 4, 256)
        field_rows(8 + 16 * j, 0, 16)
        tap_products(w3[...], fields, 8 + 16 * j, taps3, 8, 16, 8, 4, 128)
        pack(j)
        for out, stay, to in transfers(j):
            pl.when(is_source & away(to))(out.start)
            pl.when(is_source & jnp.logical_not(away(to)))(stay.start)
        return carry

    lax.fori_loop(0, 4, chunk, 0)
    for q in range(4):
        map_out[:, 16 * q : 16 * q + 16, :] = jnp.swapaxes(
            fields[4 + 16 * q : 20 + 16 * q, :, 0:128], 0, 1
        )
    for q in range(2):
        (main_in, main_own, _), (outer_in, outer_own, _) = transfers(q)[:2]
        pl.when(remote_main)(main_in.wait_recv)
        pl.when(jnp.logical_not(remote_main))(main_own.wait)
        pl.when(remote_outer)(outer_in.wait_recv)
        pl.when(jnp.logical_not(remote_outer))(outer_own.wait)
    rims = [
        (got.at[pl.ds(13, 5)], top, (down, c)),
        (got.at[pl.ds(0, 5)], bottom, (up, c)),
        (outer.at[pl.ds(1, 1)], top_outer, (down, c)),
        (outer.at[pl.ds(0, 1)], bottom_outer, (up, c)),
    ]
    rims = [copy(s, t, send_n.at[k], recv_n.at[k], to) for k, (s, t, to) in enumerate(rims)]
    for y in rims:
        y.start()
    for j in range(4):
        for out, _, to in transfers(j):
            pl.when(is_source & away(to))(out.wait_send)
    for y in rims:
        y.wait()


def coarse(half, tile, rows, rim_left, rim_right, gathered, weights, first_refine, biases):
    return pl.pallas_call(
        functools.partial(coarse_kernel, half),
        out_shape=(
            jax.ShapeDtypeStruct((64, TR, TC), BF),
            jax.ShapeDtypeStruct((18, 64, TC), BF),
            jax.ShapeDtypeStruct((2, 64, TC), BF),
            jax.ShapeDtypeStruct((5, 64, TC), BF),
            jax.ShapeDtypeStruct((1, 64, TC), BF),
            jax.ShapeDtypeStruct((5, 64, TC), BF),
            jax.ShapeDtypeStruct((1, 64, TC), BF),
        ),
        in_specs=[vmem] * 8,
        out_specs=(vmem,) + (anywhere,) * 6,
        scratch_shapes=[
            pltpu.VMEM((84, 64, 256), BF),
            pltpu.VMEM((20, 192, 256), F32),
            pltpu.VMEM((80, 64, 256), BF),
            pltpu.VMEM((24, 192, 256), F32),
            pltpu.VMEM((72, 64, 256), BF),
            pltpu.VMEM((24, 192, 128), F32),
            pltpu.VMEM((192, 192), BF),
            pltpu.VMEM((2, 64, 256), F32),
            pltpu.VMEM((64, 128), F32),
            pltpu.VMEM((64, 256), F32),
            pltpu.VMEM((2, 2, 18, 64, 128), BF),
            pltpu.VMEM((2, 2, 2, 64, 128), BF),
            pltpu.SemaphoreType.DMA((8,)),
            pltpu.SemaphoreType.DMA((2,)),
            pltpu.SemaphoreType.DMA((8,)),
            pltpu.SemaphoreType.DMA((2,)),
            pltpu.SemaphoreType.DMA((4,)),
            pltpu.SemaphoreType.DMA((4,)),
            pltpu.SemaphoreType.DMA((2,)),
            pltpu.SemaphoreType.DMA((2,)),
        ],
        compiler_params=pltpu.CompilerParams(
            collective_id=2 + half, has_side_effects=True, vmem_limit_bytes=VMEM_BYTES
        ),
    )(tile, rows, rim_left, rim_right, gathered, weights, first_refine, biases)


def mesh_place():
    return lax.axis_index("row"), lax.axis_index("col")


def spread_tables():
    lane = np.arange(128)
    source = np.arange(128)[:, None]
    main = np.stack([source == 64 * k + lane[None] // 2 for k in range(2)])
    rim = np.zeros((256, 16, 128), bool)
    for k in range(16):
        rim[:128, k] = (source == 8 * k + lane[None] // 2) & (lane[None] < 16)
        rim[128:, k] = (source == 8 * k + (lane[None] - 112) // 2) & (lane[None] >= 112)
    return main.astype(np.float32), rim.reshape(256, 2048).astype(np.float32)


def refine_kernel(place, got, outer, top, top_outer, bottom, bottom_outer, gathered,
                  first_refine, second_refine, biases, main_table, rim_table,
                  out, wide, hidden, taps, row_terms, row_part, bias):
    r, c = place()
    row0, col0 = r * TR, c * TC
    joined = first_refine[...].reshape(192, 384)
    wq = halves_joined(joined[:, 0:128], joined[:, 128:256], joined[:, 256:384], True)
    wp = jnp.concatenate(
        [
            halves_joined(*[first_refine[a, :, 128 * e : 128 * e + 128] for a in range(3)], True)
            for e in range(3)
        ],
        axis=0,
    )
    w4 = second_refine[...].reshape(192, 192)
    bias[...] = bias_columns(biases, 1, 128)
    fc = chosen_bins(gathered, col0, True)[64:128].astype(BF)
    q = jnp.dot(wq, shifted_stack(fc, 8, 256), preferred_element_type=F32)
    base = q[64:128] + bias_columns(biases, 0, 256)
    row_terms[0] = base + q[0:64] + q[128:192]
    row_terms[1] = base + q[128:192]
    row_terms[2] = base + q[0:64]
    fr = chosen_bins(gathered, row0 - 24, False)[64:128].astype(BF)
    stack = jnp.concatenate([pltpu.roll(fr, 8, 1), fr, pltpu.roll(fr, 120, 1)], axis=0)
    p = jnp.dot(wp, stack, preferred_element_type=F32)
    row_part[0] = p[0:64] + p[64:128] + p[128:192]
    row_part[1] = p[64:128] + jnp.where(c == 0, p[128:192], p[0:64])
    cols = col0 + column_offsets((64, 256))
    in_cols = (cols >= 0) & (cols < SIDE)
    at_edge = (cols < 8) | (cols >= SIDE - 8)

    def spread_main(source, first, count, at):
        for k in range(2):
            value = jnp.dot(
                source[first : first + count].reshape(count * 64, 128),
                main_table[k],
                preferred_element_type=F32,
            )
            wide[at : at + count, k, :, 0:128] = value.reshape(count, 64, 128).astype(BF)

    spread_main(top, 0, 4, 0)
    spread_main(got, 1, 16, 4)
    spread_main(bottom, 1, 4, 20)
    inner_right = lax.rem(c, 2) == 0

    def spread_rim(inside, outside, low, high, first):
        both = jnp.concatenate(
            [
                jnp.where(inner_right, inside, outside),
                jnp.where(inner_right, outside, inside),
            ],
            axis=1,
        )
        value = jnp.dot(
            both, rim_table[:, 128 * low : 128 * high], preferred_element_type=F32
        ).astype(BF)
        for k in range(high - low):
            row = first + k
            wide[row // 2, row % 2, :, 128:256] = value[:, 128 * k : 128 * k + 128]

    spread_rim(top[4], top_outer[0], 8, 16, 0)
    spread_rim(got[0], outer[0], 0, 16, 8)
    spread_rim(got[17], outer[1], 0, 16, 24)
    spread_rim(bottom[0], bottom_outer[0], 0, 8, 40)

    def hidden_rows(g, carry):
        grow0 = row0 + 8 * g - 16
        inside = in_cols & (grow0 >= 0) & (grow0 < SIDE)
        variant = jnp.where(grow0 == 0, 1, jnp.where(grow0 == SIDE - 8, 2, 0))
        shift = lax.rem(256 - 8 * g - 8, 128)
        everywhere = pltpu.roll(row_part[0], shift, 1)
        edge = pltpu.roll(row_part[1], shift, 1)
        terms = row_terms[variant]
        for k in range(8):
            row = jnp.where(at_edge, edge[:, k : k + 1], everywhere[:, k : k + 1])
            value = wide[2 * g + k // 4, (k // 2) % 2].astype(F32) + (terms + row)
            hidden[8 * g + k] = jnp.where(inside, jnp.maximum(value, 0.0), 0.0).astype(BF)
        return carry

    lax.fori_loop(0, 12, hidden_rows, 0)

    def last_products(g, carry):
        tap_products(w4, hidden, 16 * g, taps, 16 * g, 16, 8, 16, 128)
        return carry

    lax.fori_loop(0, 6, last_products, 0)

    for g in range(4):
        value = jnp.stack(
            [
                jnp.maximum(tap_sum(taps, 16 * g + k, 16, 128) + bias[...], 0.0).astype(BF)
                for k in range(16)
            ]
        )
        out[:, 16 * g : 16 * g + 16, :] = jnp.swapaxes(value, 0, 1)


def refine(place, got, outer, top, top_outer, bottom, bottom_outer, gathered,
           first_refine, second_refine, biases):
    main_table, rim_table = spread_tables()
    return pl.pallas_call(
        functools.partial(refine_kernel, place),
        out_shape=jax.ShapeDtypeStruct((64, TR, TC), BF),
        in_specs=[vmem] * 12,
        out_specs=vmem,
        scratch_shapes=[
            pltpu.VMEM((24, 2, 64, 256), BF),
            pltpu.VMEM((96, 64, 256), BF),
            pltpu.VMEM((96, 192, 128), F32),
            pltpu.VMEM((3, 64, 256), F32),
            pltpu.VMEM((2, 64, 128), F32),
            pltpu.VMEM((64, 128), F32),
        ],
        compiler_params=pltpu.CompilerParams(vmem_limit_bytes=VMEM_BYTES),
    )(got, outer, top, top_outer, bottom, bottom_outer, gathered, first_refine, second_refine, biases,
      jnp.asarray(main_table, BF), jnp.asarray(rim_table, BF))


def per_device(coarse_feats, fine_feats, pair_prior, zoom_start, coarse_weights, coarse_bias,
               refine_first, refine_second, refine_bias):
    *held, gathered = gather(coarse_feats, fine_feats, pair_prior)
    gathered = gathered.reshape(SIDE, 128)
    coarse_map, *moved = lax.cond(
        zoom_start[0] == 0,
        functools.partial(coarse, 0),
        functools.partial(coarse, 1),
        *held, gathered, coarse_weights, refine_first, coarse_bias,
    )
    refined = refine(mesh_place, *moved, gathered, refine_first, refine_second, refine_bias)
    return coarse_map, refined


def solution(mesh):
    return jax.shard_map(
        per_device,
        mesh=mesh,
        in_specs=(
            P(None, ("row", "col")),
            P(None, ("row", "col")),
            P(None, "row", "col"),
            P(),
            P(),
            P(),
            P(),
            P(),
            P(),
        ),
        out_specs=(P(None, "row", "col"), P(None, "row", "col")),
        check_vma=False,
    )
```

time: 111 us -> 81.4 us (0.73)
  the two profiles are of different devices: /device:TPU:1 before, /device:TPU:0 now
where the time goes in v2:
time: 81.4 us; the launch traced here: 81.2 us
  Pallas kernels  75.9 us (93%)
  local copies, waits for them, and re-layouts  4.35 us (5%)
    pallas_call x1, Pallas kernels, coarse(): pl.pallas_call(functools.partial(coarse_kernel, half), out_shape=(jax.Sha...  46 us
    pallas_call x1, Pallas kernels, gather(): pl.pallas_call(gather_kernel, out_shape=(jax.ShapeDtypeStruct((TR, 64, TC...  18.2 us
    pallas_call x1, Pallas kernels, refine(): pl.pallas_call(functools.partial(refine_kernel, place), out_shape=jax.Sha...  11.7 us
    unnamed x15, local copies, waits for them, and re-layouts  4.35 us

profile of v2, /device:TPU:0, one launch (start us, length us, event | category | flops | bytes accessed | tf_op | source)
XLA Modules:
  0.0 81.2 jit_solution(12844561843058673325)
XLA Ops:
  0.6 0.0 copy-start.5
  0.6 0.6 copy-done.5
  1.3 0.0 copy-start.3
  1.3 0.7 copy-done.3
  2.0 0.0 copy-start.4
  2.0 0.7 copy.13.coarse_feats
  2.7 0.0 copy-done.4
  2.7 0.7 copy.14.fine_feats
  3.4 0.0 copy-start
  3.4 0.0 copy-start.1
  3.4 18.2 %shard_map.122 = (bf16[64,64,128]{2,1,0:T(8,128)(2,1)S(1)}, bf16[2,10,64,128]{3,2,1,0:T(8,128)(2,1)S(1)}, bf16[12,64,128]{2,1,0:T(8,128)(2,1)S(1)}, bf16[12,64,1...) custom-call(bf16[64,8]{1,0:T(8,128)(2,1)} %copy.13.coarse_feats, bf16[64,8]{1,0:T(8,128)(2,1)} %copy.14.fine_feats, ...), custom_call_target="tpu_custom_call" | custom-call | tf_op jit(solution)/shard_map/pallas_call | solution.py:184
  21.6 0.0 copy-start.2
  21.6 0.0 copy-done
  21.6 0.0 copy-done.1
  21.6 0.7 copy-done.2
  22.3 46.2 %conditional.1 = ((bf16[64,64,128]{2,1,0:T(8,128)(2,1)S(1)}, bf16[18,64,128]{2,1,0:T(8,128)(2,1)}, bf16[2,64,128]{2,1,0:T(8,128)(2,1)S(1)}, bf16[5,64,128]{2,1,0...) conditional(s32[]{:T(128)} %bitcast, ...), branch_computations={%region_0.0_spmd, %region_1.0_spmd} | conditional | bytes 8 | solution.py:616
  22.3 46.0 %branch_1_fun.1 = (bf16[64,64,128]{2,1,0:T(8,128)(2,1)S(1)}, bf16[18,64,128]{2,1,0:T(8,128)(2,1)}, bf16[2,64,128]{2,1,0:T(8,128)(2,1)S(1)}, bf16[5,64,128]{2,1,0...) custom-call(bf16[64,64,128]{2,1,0:T(8,128)(2,1)S(1)} %get-tuple-elemen, ...), custom_call_target="tpu_custom_call" | custom-call | tf_op jit(solution)/shard_map/cond/branch_1_fun/pallas_call | solution.py:438
  68.5 11.7 %shard_map.123 = bf16[64,64,128]{2,1,0:T(8,128)(2,1)} custom-call(bf16[18,64,128]{2,1,0:T(8,128)(2,1)} %get-tuple-element.68.got, bf16[2,64,128]{2,1,0:T(8,128)(2,1)S(1)} %get-tuple-element.69.outer, bf16[5,64,128]{2,1,0:T(8,128)(2,1)S(1)} %get-tuple-element.70.top, bf16[1,64,128]{2,1,0:T(8,128)(2,1)S(1)} %get-tuple-element.71.top_outer, ...), custom_call_target="tpu_custom_call" | custom-call | tf_op jit(solution)/shard_map/pallas_call | solution.py:594
  80.2 1.0 %copy.30 = bf16[64,64,128]{2,1,0:T(8,128)(2,1)} copy(bf16[64,64,128]{2,1,0:T(8,128)(2,1)S(1)} %get-tuple-element.90) | data formatting | bytes 2097152
Async XLA Ops:
  0.6 0.7 copy-start.5
  1.3 0.7 copy-start.3
  2.0 0.7 copy-start.4
  3.4 18.2 %copy-start = (bf16[3,64,384]{2,1,0:T(8,128)(2,1)S(1)}, bf16[3,64,384]{2,1,0:T(8,128)(2,1)}, u32[]{:S(2)}) copy-start(bf16[3,64,384]{2,1,0:T(8,128)(2,1)} %first_refine.1) | copy-start | bytes 442372
  3.4 18.2 %copy-start.1 = (bf16[2,3,64,192]{3,2,1,0:T(8,128)(2,1)S(1)}, bf16[2,3,64,192]{3,2,1,0:T(8,128)(2,1)}, u32[]{:S(2)}) copy-start(bf16[2,3,64,192]{3,2,1,0:T(8,128)(2,1)} %param.17) | copy-start | bytes 442372
  21.6 0.7 copy-start.2

commit v3 on v2

v3 whole, which is shorter than its diff:
```python
import functools

import jax
import jax.numpy as jnp
import numpy as np
from jax import lax
from jax.experimental import pallas as pl
from jax.experimental.pallas import tpu as pltpu
from jax.sharding import PartitionSpec as P

BF = jnp.bfloat16
F32 = jnp.float32
MESH = pl.DeviceIdType.MESH
VMEM_BYTES = 48 << 20
SIDE = 1024
ROWS, COLS = 16, 8
TR, TC = 64, 128

vmem = pl.BlockSpec(memory_space=pltpu.VMEM)
anywhere = pl.BlockSpec(memory_space=pl.ANY)


def lanes_of(shape):
    return lax.broadcasted_iota(jnp.int32, shape, len(shape) - 1)


def column_offsets(shape):
    lane = lanes_of(shape)
    return jnp.where(lane < 192, lane, lane - 256)


def shifted_stack(x, spacing, width):
    return jnp.concatenate(
        [
            pltpu.roll(x, spacing, 1)[:, :width],
            x[:, :width],
            pltpu.roll(x, 256 - spacing, 1)[:, :width],
        ],
        axis=0,
    )


def tap_products(w, source, first, target, into, count, group, spacing, width):
    for g in range(count // group):
        base = first + g * group
        stack = jnp.concatenate(
            [shifted_stack(source[base + t], spacing, width) for t in range(group)], axis=1
        )
        product = jnp.dot(w, stack, preferred_element_type=F32)
        for t in range(group):
            target[into + g * group + t] = product[:, t * width : (t + 1) * width]


def carry_taps(target, spacing):
    last = target.shape[0] - 2 * spacing
    for t in range(2 * spacing):
        target[t, 0:64] = target[last + t, 0:64]
        if t >= spacing:
            target[t, 64:128] = target[last + t, 64:128]


def tap_sum(target, i, spacing, width):
    return (
        target[i, 0:64, 0:width]
        + target[i + spacing, 64:128, 0:width]
        + target[i + 2 * spacing, 128:192, 0:width]
    )


def bias_columns(bias, layer, width):
    row = jnp.broadcast_to(bias[layer : layer + 1, :], (128, 64))
    column = jnp.transpose(row)
    return column if width == 128 else jnp.concatenate([column, column], axis=1)


def halves_joined(a, b, c, upper):
    low = lanes_of(a.shape) < 64
    if upper:
        first = jnp.where(low, pltpu.roll(a, 64, 1), b)
        return jnp.concatenate([first, pltpu.roll(c, 64, 1)[:, :64]], axis=1)
    first = jnp.where(low, a, pltpu.roll(b, 64, 1))
    return jnp.concatenate([first, c[:, :64]], axis=1)


def gather_kernel(coarse_feats, fine_feats, prior, tile, rows, rim_left, rim_right, gathered,
                  feats, left, right, send, recv, send_a, recv_a, send_b, recv_b, own):
    r, c = lax.axis_index("row"), lax.axis_index("col")
    up, down = lax.rem(r + ROWS - 1, ROWS), lax.rem(r + 1, ROWS)
    west, east = lax.rem(c + COLS - 1, COLS), lax.rem(c + 1, COLS)
    has_up, has_down, has_west, has_east = r > 0, r < ROWS - 1, c > 0, c < COLS - 1
    barrier = pltpu.get_barrier_semaphore()

    def greet(to):
        pl.semaphore_signal(barrier, 1, device_id=to, device_id_type=MESH)

    for d in range(1, COLS):
        greet((r, lax.rem(c + d, COLS)))
    for d in range(1, ROWS):
        greet((lax.rem(r + d, ROWS), c))
    peers = COLS - 1 + ROWS - 1
    for a, has_a in ((up, has_up), (down, has_down)):
        for b, has_b in ((west, has_west), (east, has_east)):
            pl.when(has_a & has_b)(functools.partial(greet, (a, b)))
            peers = peers + jnp.where(has_a & has_b, 1, 0)

    both = jnp.concatenate([coarse_feats[...], fine_feats[...]], axis=0).astype(F32)
    feats[...] = jnp.transpose(both).astype(BF)
    for q in range(4):
        tile[16 * q : 16 * q + 16] = jnp.swapaxes(prior[:, 16 * q : 16 * q + 16, :], 0, 1)
    part = lanes_of((64, 128)) // 16

    def pack(q, carry):
        low = tile[8 * q]
        high = pltpu.roll(low, 16, 1)
        for k in range(1, 8):
            x = tile[8 * q + k]
            low = jnp.where(part == k, pltpu.roll(x, 16 * k, 1), low)
            high = jnp.where(part == k, pltpu.roll(x, (16 * k + 16) % 128, 1), high)
        left[q] = low
        right[q] = high
        return carry

    def copy(source, target, out_sem, in_sem, to):
        return pltpu.make_async_remote_copy(
            src_ref=source,
            dst_ref=target,
            send_sem=out_sem,
            recv_sem=in_sem,
            device_id=to,
            device_id_type=MESH,
        )

    pl.semaphore_wait(barrier, peers)
    place = r * COLS + c
    mine = pltpu.make_async_copy(feats, gathered.at[place], own)
    mine.start()
    first = [
        copy(feats, gathered.at[place], send_a.at[d], recv_a.at[d], (r, lax.rem(c + d, COLS)))
        for d in range(1, COLS)
    ]
    for x in first:
        x.start()
    lax.fori_loop(0, 8, pack, 0)
    rims = [
        (right, rim_left.at[pl.ds(2, 8)], (r, east), has_east, has_west),
        (left, rim_right.at[pl.ds(2, 8)], (r, west), has_west, has_east),
        (tile.at[pl.ds(54, 10)], rows.at[0], (down, c), has_down, has_up),
        (tile.at[pl.ds(0, 10)], rows.at[1], (up, c), has_up, has_down),
        (right.at[pl.ds(6, 2)], rim_left.at[pl.ds(0, 2)], (down, east),
         has_down & has_east, has_up & has_west),
        (right.at[pl.ds(0, 2)], rim_left.at[pl.ds(10, 2)], (up, east),
         has_up & has_east, has_down & has_west),
        (left.at[pl.ds(6, 2)], rim_right.at[pl.ds(0, 2)], (down, west),
         has_down & has_west, has_up & has_east),
        (left.at[pl.ds(0, 2)], rim_right.at[pl.ds(10, 2)], (up, west),
         has_up & has_west, has_down & has_east),
    ]
    rims = [
        (copy(s, t, send.at[k], recv.at[k], to), out, into)
        for k, (s, t, to, out, into) in enumerate(rims)
    ]
    for x, out, _ in rims:
        pl.when(out)(x.start)
    mine.wait()
    for x in first:
        x.wait_recv()
    block = gathered.at[pl.ds(r * COLS, COLS)]
    second = [
        copy(block, block, send_b.at[d], recv_b.at[d], (lax.rem(r + d, ROWS), c))
        for d in range(1, ROWS)
    ]
    for x in second:
        x.start()
    for x in first:
        x.wait_send()
    for x, out, into in rims:
        pl.when(out)(x.wait_send)
        pl.when(into)(x.wait_recv)
    for x in second:
        x.wait()


def gather(coarse_feats, fine_feats, prior):
    return pl.pallas_call(
        gather_kernel,
        out_shape=(
            jax.ShapeDtypeStruct((TR, 64, TC), BF),
            jax.ShapeDtypeStruct((2, 10, 64, TC), BF),
            jax.ShapeDtypeStruct((12, 64, TC), BF),
            jax.ShapeDtypeStruct((12, 64, TC), BF),
            jax.ShapeDtypeStruct((ROWS * COLS, 8, TC), BF),
        ),
        in_specs=[vmem] * 3,
        out_specs=(vmem,) + (anywhere,) * 4,
        scratch_shapes=[
            pltpu.VMEM((8, TC), BF),
            pltpu.VMEM((8, 64, TC), BF),
            pltpu.VMEM((8, 64, TC), BF),
            pltpu.SemaphoreType.DMA((8,)),
            pltpu.SemaphoreType.DMA((8,)),
            pltpu.SemaphoreType.DMA((COLS,)),
            pltpu.SemaphoreType.DMA((COLS,)),
            pltpu.SemaphoreType.DMA((ROWS,)),
            pltpu.SemaphoreType.DMA((ROWS,)),
            pltpu.SemaphoreType.DMA,
        ],
        compiler_params=pltpu.CompilerParams(
            collective_id=1, has_side_effects=True, vmem_limit_bytes=VMEM_BYTES
        ),
    )(coarse_feats, fine_feats, prior)


def chosen_bins(gathered, first, ring):
    lanes = 256 if ring else 128
    shape = (SIDE, lanes)
    wanted = first + (column_offsets(shape) if ring else lanes_of(shape))
    picked = lax.broadcasted_iota(jnp.int32, shape, 0) == wanted
    return lax.dot_general(
        gathered[...],
        jnp.where(picked, 1.0, 0.0).astype(BF),
        (((0,), (0,)), ((), ())),
        preferred_element_type=F32,
    )


def spread_tables():
    lane = np.arange(128)
    source = np.arange(128)[:, None]
    main = np.stack([source == 64 * k + lane[None] // 2 for k in range(2)])
    rim = np.zeros((256, 16, 128), bool)
    for k in range(16):
        rim[:128, k] = (source == 8 * k + lane[None] // 2) & (lane[None] < 16)
        rim[128:, k] = (source == 8 * k + (lane[None] - 112) // 2) & (lane[None] >= 112)
    return main.astype(np.float32), rim.reshape(256, 2048).astype(np.float32)


def decoder_kernel(half, tile, rows, rim_left, rim_right, gathered, weights, first_refine,
                   second_refine, coarse_bias, refine_bias, main_table, rim_table,
                   map_out, refined,
                   x, taps1, hidden, taps2, fields, taps3, w3, bias, fr, fc, pieces,
                   got, sides, top, bottom, side_in, wide, fine, taps4, row_terms, row_part,
                   send, recv, own, send_n, recv_n):
    r, c = lax.axis_index("row"), lax.axis_index("col")
    base_r, base_c = half * (ROWS // 2), half * (COLS // 2)
    up, down = lax.rem(r + ROWS - 1, ROWS), lax.rem(r + 1, ROWS)
    west, east = lax.rem(c + COLS - 1, COLS), lax.rem(c + 1, COLS)
    has_up, has_down, has_west, has_east = r > 0, r < ROWS - 1, c > 0, c < COLS - 1
    from_r, from_c = base_r + r // 2, base_c + c // 2
    remote_main = (from_r != r) | (from_c != c)
    is_source = (r >= base_r) & (r < base_r + ROWS // 2) & (c >= base_c) & (c < base_c + COLS // 2)
    local_r, local_c = r - base_r, c - base_c

    def main_to(t, h):
        return 2 * local_r + t, 2 * local_c + h

    def away(to):
        return (to[0] != r) | (to[1] != c)

    barrier = pltpu.get_barrier_semaphore()

    def greet(to):
        pl.semaphore_signal(barrier, 1, device_id=to, device_id_type=MESH)

    around = [
        ((up, c), has_up),
        ((down, c), has_down),
        ((r, west), has_west),
        ((r, east), has_east),
        ((up, west), has_up & has_west),
        ((up, east), has_up & has_east),
        ((down, west), has_down & has_west),
        ((down, east), has_down & has_east),
    ]
    met = around + [((from_r, from_c), remote_main)]
    met += [(main_to(t, k), is_source & away(main_to(t, k))) for t in range(2) for k in range(2)]
    peers = 0
    for to, there in met:
        pl.when(there)(functools.partial(greet, to))
        peers = peers + jnp.where(there, 1, 0)

    def copy(source, target, out_sem, in_sem, to):
        return pltpu.make_async_remote_copy(
            src_ref=source,
            dst_ref=target,
            send_sem=out_sem,
            recv_sem=in_sem,
            device_id=to,
            device_id_type=MESH,
        )

    def piece(j, k):
        t, q = j // 2, lax.rem(j, 2)
        return copy(pieces.at[k, t, pl.ds(8 * q, 8)], got.at[pl.ds(8 * q, 8)],
                    send.at[2 * j + k], recv.at[q], main_to(t, k))

    def stay(j, k):
        t, q = j // 2, lax.rem(j, 2)
        return pltpu.make_async_copy(
            pieces.at[k, t, pl.ds(8 * q, 8)], got.at[pl.ds(8 * q, 8)], own.at[q]
        )

    w1 = weights[0].reshape(192, 192)
    w2 = weights[1].reshape(192, 192)
    joined = first_refine[...].reshape(192, 384)
    w3[...] = halves_joined(joined[:, 0:128], joined[:, 128:256], joined[:, 256:384], False)
    bias[0] = bias_columns(coarse_bias, 0, 256)
    bias[1] = bias_columns(coarse_bias, 1, 256)
    row0, col0 = r * TR, c * TC
    fr[...] = chosen_bins(gathered, row0 - 16, False)[0:64]
    fc[...] = chosen_bins(gathered, col0, True)[0:64]
    cols = col0 + column_offsets((64, 256))
    in_cols = (cols >= 0) & (cols < SIDE)
    half_c, half_r = lax.rem(c, COLS // 2) * TC, lax.rem(r, ROWS // 2) * TR
    cols_q = half_c + column_offsets((64, 256))
    in_quarter = (cols_q >= 0) & (cols_q < SIDE // 2)
    low_half = lanes_of((64, 128)) < 64

    def pair_row(q, k, at, body, shift):
        rim = jnp.where(
            low_half,
            pltpu.roll(rim_right[q], (128 - 16 * k) % 128, 1),
            pltpu.roll(rim_left[q], 112 - 16 * k, 1),
        )
        prior = jnp.concatenate([body, rim], axis=1).astype(F32)
        value = prior + (fc[...] + shift[:, k : k + 1])
        grow = row0 + 8 * q + k - 16
        inside = in_cols & (grow >= 0) & (grow < SIDE)
        x[at] = jnp.where(inside, value, 0.0).astype(BF)

    def features_at(q):
        return pltpu.roll(fr[...], lax.rem(256 - 8 * q, 128), 1)

    def rim_rows(side):
        for k in range(10):
            row = 64 + k if side else k - 10
            q = (row + 16) // 8
            pair_row(q, row % 8, row + 10, rows[side, k], features_at(q))

    def own_rows(g):
        shift = features_at(g + 2)
        for k in range(8):
            pair_row(g + 2, k, 8 * g + k + 10, tile[8 * g + k], shift)

    def hidden_rows(first, taken, count):
        for t in range(count):
            at = first + t
            grow = row0 + at - 8
            value = jnp.maximum(tap_sum(taps1, taken + t, 2, 256) + bias[0], 0.0)
            inside = in_cols & (grow >= 0) & (grow < SIDE)
            hidden[at] = jnp.where(inside, value, 0.0).astype(BF)

    def field_rows(first, taken, count):
        for t in range(count):
            at = first + t
            qrow = half_r + at - 4
            value = jnp.maximum(tap_sum(taps2, taken + t, 4, 256) + bias[1], 0.0)
            inside = in_quarter & (qrow >= 0) & (qrow < SIDE // 2)
            fields[at] = jnp.where(inside, value, 0.0).astype(BF)

    def pack(j):
        t, q = j // 2, lax.rem(j, 2)
        for k in range(0, 16, 2):
            v = tap_sum(taps3, k, 4, 128).astype(BF)
            u = tap_sum(taps3, k + 1, 4, 128).astype(BF)
            at = 8 * q + k // 2
            pieces[0, t, at] = jnp.where(low_half, v, pltpu.roll(u, 64, 1))
            pieces[1, t, at] = jnp.where(low_half, pltpu.roll(v, 64, 1), u)

    rim_rows(0)

    def early_rows(g, carry):
        own_rows(g)
        return carry

    lax.fori_loop(0, 4, early_rows, 0)
    tap_products(w1, x, 0, taps1, 0, 20, 10, 2, 256)
    hidden_rows(0, 0, 16)
    tap_products(w2, hidden, 0, taps2, 8, 16, 8, 4, 256)
    field_rows(0, 8, 8)
    tap_products(w3[...], fields, 0, taps3, 16, 8, 8, 4, 128)
    pl.semaphore_wait(barrier, peers)

    def chunk(j, carry):
        @pl.when((j == 1) | (j == 2))
        def _():
            own_rows(2 * j + 2)
            own_rows(2 * j + 3)

        pl.when(j == 3)(lambda: rim_rows(1))
        carry_taps(taps1, 2)
        carry_taps(taps2, 4)
        carry_taps(taps3, 4)
        tap_products(w1, x, 20 + 16 * j, taps1, 4, 16, 8, 2, 256)
        hidden_rows(16 + 16 * j, 0, 16)
        tap_products(w2, hidden, 16 + 16 * j, taps2, 8, 16, 8, 4, 256)
        field_rows(8 + 16 * j, 0, 16)
        tap_products(w3[...], fields, 8 + 16 * j, taps3, 8, 16, 8, 4, 128)
        pack(j)
        for k in range(2):
            pl.when(is_source & away(main_to(j // 2, k)))(lambda k=k: piece(j, k).start())
            pl.when(is_source & jnp.logical_not(away(main_to(j // 2, k))))(
                lambda k=k: stay(j, k).start()
            )
        return carry

    lax.fori_loop(0, 4, chunk, 0)
    for q in range(4):
        map_out[:, 16 * q : 16 * q + 16, :] = jnp.swapaxes(
            fields[4 + 16 * q : 20 + 16 * q, :, 0:128], 0, 1
        )

    wq = halves_joined(joined[:, 0:128], joined[:, 128:256], joined[:, 256:384], True)
    wp = jnp.concatenate(
        [
            halves_joined(*[first_refine[a, :, 128 * e : 128 * e + 128] for a in range(3)], True)
            for e in range(3)
        ],
        axis=0,
    )
    w4 = second_refine[...].reshape(192, 192)
    fine_c = chosen_bins(gathered, col0, True)[64:128].astype(BF)
    terms = jnp.dot(wq, shifted_stack(fine_c, 8, 256), preferred_element_type=F32)
    base = terms[64:128] + bias_columns(refine_bias, 0, 256)
    row_terms[0] = base + terms[0:64] + terms[128:192]
    row_terms[1] = base + terms[128:192]
    row_terms[2] = base + terms[0:64]
    fine_r = chosen_bins(gathered, row0 - 24, False)[64:128].astype(BF)
    stack = jnp.concatenate([pltpu.roll(fine_r, 8, 1), fine_r, pltpu.roll(fine_r, 120, 1)], axis=0)
    terms = jnp.dot(wp, stack, preferred_element_type=F32)
    row_part[0] = terms[0:64] + terms[64:128] + terms[128:192]
    row_part[1] = terms[64:128] + jnp.where(c == 0, terms[128:192], terms[0:64])
    bias[0] = bias_columns(refine_bias, 1, 256)

    def spread_main(source, first, count, at):
        for k in range(2):
            value = jnp.dot(
                source[first : first + count].reshape(count * 64, 128),
                main_table[k],
                preferred_element_type=F32,
            )
            wide[at : at + count, k, :, 0:128] = value.reshape(count, 64, 128).astype(BF)

    part = lanes_of((64, 128)) // 8
    for q in range(2):
        pl.when(remote_main)(lambda: piece(q, 0).wait_recv())
        pl.when(jnp.logical_not(remote_main))(lambda: stay(q, 0).wait())
        low = high = None
        for k in range(16):
            v = got[8 * q + k // 2]
            first = (8 * k - 64 * (k % 2)) % 128
            moved, other = pltpu.roll(v, first, 1), pltpu.roll(v, (first - 56) % 128, 1)
            low = moved if k == 0 else jnp.where(part == k, moved, low)
            high = other if k == 0 else jnp.where(part == k, other, high)
        sides[0, q] = low
        sides[1, q] = high
    rims = [
        (got.at[pl.ds(12, 4)], top, (down, c), has_down, has_up),
        (got.at[pl.ds(0, 4)], bottom, (up, c), has_up, has_down),
        (sides.at[0], side_in.at[1, pl.ds(1, 2)], (r, west), has_west, has_east),
        (sides.at[1], side_in.at[0, pl.ds(1, 2)], (r, east), has_east, has_west),
        (sides.at[0, 1], side_in.at[1, 0], (down, west),
         has_down & has_west, has_up & has_east),
        (sides.at[1, 1], side_in.at[0, 0], (down, east),
         has_down & has_east, has_up & has_west),
        (sides.at[0, 0], side_in.at[1, 3], (up, west),
         has_up & has_west, has_down & has_east),
        (sides.at[1, 0], side_in.at[0, 3], (up, east),
         has_up & has_east, has_down & has_west),
    ]
    rims = [
        (copy(s, t, send_n.at[k], recv_n.at[k], to), out, into)
        for k, (s, t, to, out, into) in enumerate(rims)
    ]
    for y, out, _ in rims:
        pl.when(out)(y.start)

    offsets = column_offsets((64, 256)) + col0
    inside_of = [(offsets >= 0) & (offsets < SIDE)]
    edge_of = [(offsets < 8) | (offsets >= SIDE - 8)]

    def fine_rows(g, at):
        lanes = slice(at, at + 128)
        grow0 = row0 + 8 * g - 16
        inside = inside_of[0][:, lanes] & (grow0 >= 0) & (grow0 < SIDE)
        variant = jnp.where(grow0 == 0, 1, jnp.where(grow0 == SIDE - 8, 2, 0))
        shift = lax.rem(256 - 8 * g - 8, 128)
        everywhere = pltpu.roll(row_part[0], shift, 1)
        edge = pltpu.roll(row_part[1], shift, 1)
        column_terms = row_terms[variant, :, lanes]
        for k in range(8):
            row = jnp.where(edge_of[0][:, lanes], edge[:, k : k + 1], everywhere[:, k : k + 1])
            value = wide[2 * g + k // 4, (k // 2) % 2, :, lanes].astype(F32) + (column_terms + row)
            fine[8 * g + k, :, lanes] = jnp.where(inside, jnp.maximum(value, 0.0), 0.0).astype(BF)

    def own_fine_rows(g, carry):
        fine_rows(g, 0)
        return carry

    def side_fine_rows(g, carry):
        fine_rows(g, 128)
        return carry

    spread_main(got, 0, 16, 4)
    lax.fori_loop(2, 10, own_fine_rows, 0)
    for j in range(4):
        for k in range(2):
            pl.when(is_source & away(main_to(j // 2, k)))(lambda: piece(j, k).wait_send())
    for y, out, into in rims:
        pl.when(out)(y.wait_send)
        pl.when(into)(y.wait_recv)
    spread_main(top, 0, 4, 0)
    spread_main(bottom, 0, 4, 20)

    def spread_rim(tile_at, low, high, first):
        both = jnp.concatenate(
            [
                jnp.where(has_east, side_in[1, tile_at].astype(F32), 0.0),
                jnp.where(has_west, side_in[0, tile_at].astype(F32), 0.0),
            ],
            axis=1,
        ).astype(BF)
        value = jnp.dot(
            both, rim_table[:, 128 * low : 128 * high], preferred_element_type=F32
        ).astype(BF)
        for k in range(high - low):
            row = first + k
            wide[row // 2, row % 2, :, 128:256] = value[:, 128 * k : 128 * k + 128]

    spread_rim(0, 8, 16, 0)
    spread_rim(1, 0, 16, 8)
    spread_rim(2, 0, 16, 24)
    spread_rim(3, 0, 8, 40)
    for g in (0, 1, 10, 11):
        fine_rows(g, 0)
    lax.fori_loop(0, 12, side_fine_rows, 0)

    def last_products(g, carry):
        tap_products(w4, fine, 16 * g, taps4, 16 * g, 16, 8, 16, 128)
        return carry

    lax.fori_loop(0, 6, last_products, 0)
    for g in range(4):
        value = jnp.stack(
            [
                jnp.maximum(tap_sum(taps4, 16 * g + k, 16, 128) + bias[0, :, 0:128], 0.0).astype(BF)
                for k in range(16)
            ]
        )
        refined[:, 16 * g : 16 * g + 16, :] = jnp.swapaxes(value, 0, 1)


def decoder(half, tile, rows, rim_left, rim_right, gathered, weights, first_refine,
            second_refine, coarse_bias, refine_bias, main_table, rim_table):
    return pl.pallas_call(
        functools.partial(decoder_kernel, half),
        out_shape=(
            jax.ShapeDtypeStruct((64, TR, TC), BF),
            jax.ShapeDtypeStruct((64, TR, TC), BF),
        ),
        in_specs=[vmem] * 12,
        out_specs=(vmem, vmem),
        scratch_shapes=[
            pltpu.VMEM((84, 64, 256), BF),
            pltpu.VMEM((20, 192, 256), F32),
            pltpu.VMEM((80, 64, 256), BF),
            pltpu.VMEM((24, 192, 256), F32),
            pltpu.VMEM((72, 64, 256), BF),
            pltpu.VMEM((24, 192, 128), F32),
            pltpu.VMEM((192, 192), BF),
            pltpu.VMEM((2, 64, 256), F32),
            pltpu.VMEM((64, 128), F32),
            pltpu.VMEM((64, 256), F32),
            pltpu.VMEM((2, 2, 16, 64, 128), BF),
            pltpu.VMEM((16, 64, 128), BF),
            pltpu.VMEM((2, 2, 64, 128), BF),
            pltpu.VMEM((4, 64, 128), BF),
            pltpu.VMEM((4, 64, 128), BF),
            pltpu.VMEM((2, 4, 64, 128), BF),
            pltpu.VMEM((24, 2, 64, 256), BF),
            pltpu.VMEM((96, 64, 256), BF),
            pltpu.VMEM((96, 192, 128), F32),
            pltpu.VMEM((3, 64, 256), F32),
            pltpu.VMEM((2, 64, 128), F32),
            pltpu.SemaphoreType.DMA((8,)),
            pltpu.SemaphoreType.DMA((2,)),
            pltpu.SemaphoreType.DMA((2,)),
            pltpu.SemaphoreType.DMA((8,)),
            pltpu.SemaphoreType.DMA((8,)),
        ],
        compiler_params=pltpu.CompilerParams(
            collective_id=2 + half, has_side_effects=True, vmem_limit_bytes=VMEM_BYTES
        ),
    )(tile, rows, rim_left, rim_right, gathered, weights, first_refine,
      second_refine, coarse_bias, refine_bias, main_table, rim_table)


def per_device(coarse_feats, fine_feats, pair_prior, zoom_start, coarse_weights, coarse_bias,
               refine_first, refine_second, refine_bias):
    *held, gathered = gather(coarse_feats, fine_feats, pair_prior)
    gathered = gathered.reshape(SIDE, 128)
    main_table, rim_table = spread_tables()
    return lax.cond(
        zoom_start[0] == 0,
        functools.partial(decoder, 0),
        functools.partial(decoder, 1),
        *held, gathered, coarse_weights, refine_first, refine_second, coarse_bias, refine_bias,
        jnp.asarray(main_table, BF), jnp.asarray(rim_table, BF),
    )


def solution(mesh):
    return jax.shard_map(
        per_device,
        mesh=mesh,
        in_specs=(
            P(None, ("row", "col")),
            P(None, ("row", "col")),
            P(None, "row", "col"),
            P(),
            P(),
            P(),
            P(),
            P(),
            P(),
        ),
        out_specs=(P(None, "row", "col"), P(None, "row", "col")),
        check_vma=False,
    )
```

time: 81.4 us -> 75.7 us (0.930)
  the two profiles are of different devices: /device:TPU:0 before, /device:TPU:18 now
where the time goes in v3:
time: 75.7 us; the launch traced here: 75.4 us
  Pallas kernels  67.1 us (89%)
  local copies, waits for them, and re-layouts  7.32 us (10%)
    pallas_call x1, Pallas kernels, decoder(): pl.pallas_call(functools.partial(decoder_kernel, half), out_shape=(jax.Sh...  47.6 us
    pallas_call x1, Pallas kernels, gather(): pl.pallas_call(gather_kernel, out_shape=(jax.ShapeDtypeStruct((TR, 64, TC...  19.5 us
    unnamed x20, local copies, waits for them, and re-layouts  7.32 us

profile of v3, /device:TPU:18, one launch (start us, length us, event | category | flops | bytes accessed | tf_op | source)
XLA Modules:
  0.0 75.4 jit_solution(4414629345383240360)
XLA Ops:
  0.6 0.0 copy-start.7
  0.6 0.6 copy-done.7
  1.3 0.0 copy-start.5
  1.3 0.7 copy-done.5
  2.0 0.0 copy-start.6
  2.0 0.1 copy.17.coarse_feats
  2.1 0.6 copy-done.6
  2.7 0.1 copy.18.fine_feats
  2.8 0.0 copy-start
  2.8 1.2 %copy-done = bf16[64,64,128]{2,1,0:T(8,128)(2,1)S(1)} copy-done((bf16[64,64,128]{2,1,0:T(8,128)(2,1)S(1)}, bf16[64,64,128]{2,1,0:T(8,128)(2,1)}, u32[]{:S(2)}) %copy-start) | copy-done | bytes 1048600
  4.0 0.0 copy-start.1
  4.0 0.0 copy-start.4
  4.0 19.5 %shard_map.126 = (bf16[64,64,128]{2,1,0:T(8,128)(2,1)S(1)}, bf16[2,10,64,128]{3,2,1,0:T(8,128)(2,1)S(1)}, bf16[12,64,128]{2,1,0:T(8,128)(2,1)S(1)}, bf16[12,64,1...) custom-call(bf16[64,8]{1,0:T(8,128)(2,1)S(1)} %copy.17.coarse_feats, bf16[64,8]{1,0:T(8,128)(2,1)S(1)} %copy.18.fine_feats, ...), custom_call_target="tpu_custom_call" | custom-call | tf_op jit(solution)/shard_map/pallas_call | solution.py:184
  23.6 0.0 copy-start.3
  23.6 0.0 copy-done.1
  23.6 0.0 copy-done.4
  23.6 0.7 copy-done.3
  24.3 47.8 %conditional.1 = ((bf16[64,64,128]{2,1,0:T(8,128)(2,1)}, bf16[64,64,128]{2,1,0:T(8,128)(2,1)})) conditional(s32[]{:T(128)} %bitcast, (bf16[64,64,128]{2,1,0:T(8,128)(2,1)S(1)}, bf16[2,10,64,128]{3,2,1,0:T(8,128)(2,1)S(1)}, bf16[12,64,128]{2,1,0:T(8,128)(2,1)S(1)}, bf16[12,64,128]{2,1,0:T(8,128)(2,1)S(1)}, bf16[1024,128]{1,0:T(8,128)(2,1)S(1)}, ...), branch_computations={%region_0.0_spmd, %region_1.0_spmd} | conditional | bytes 8 | solution.py:602
  24.3 47.6 %branch_1_fun.1 = (bf16[64,64,128]{2,1,0:T(8,128)(2,1)}, bf16[64,64,128]{2,1,0:T(8,128)(2,1)}) custom-call(bf16[64,64,128]{2,1,0:T(8,128)(2,1)S(1)} %get-tuple-element.60.tile, bf16[2,10,64,128]{3,2,1,0:T(8,128)(2,1)S(1)} %get-tuple-element.61.rows, bf16[12,64,128]{2,1,0:T(8,128)(2,1)S(1)} %get-tuple-element.62.rim_left, ...), custom_call_target="tpu_custom_call" | custom-call | tf_op jit(solution)/shard_map/cond/branch_1_fun/pallas_call | solution.py:554
  72.1 0.0 copy-start.2
  72.1 2.4 %copy.25 = bf16[64,64,128]{2,1,0:T(8,128)(2,1)} copy(bf16[64,64,128]{2,1,0:T(8,128)(2,1)} %get-tuple-element.96) | data formatting | bytes 2097152
  74.4 0.0 copy-done.2
  74.5 1.0 %copy.26 = bf16[64,64,128]{2,1,0:T(8,128)(2,1)} copy(bf16[64,64,128]{2,1,0:T(8,128)(2,1)S(1)} %copy-done.2) | data formatting | bytes 2097152
Async XLA Ops:
  0.6 0.7 copy-start.7
  1.3 0.7 copy-start.5
  2.0 0.7 copy-start.6
  2.8 1.2 %copy-start = (bf16[64,64,128]{2,1,0:T(8,128)(2,1)S(1)}, bf16[64,64,128]{2,1,0:T(8,128)(2,1)}, u32[]{:S(2)}) copy-start(bf16[64,64,128]{2,1,0:T(8,128)(2,1)} %prior.1) | copy-start | bytes 3145732
  4.0 19.6 %copy-start.1 = (bf16[256,2048]{1,0:T(8,128)(2,1)S(1)}, bf16[256,2048]{1,0:T(8,128)(2,1)}, u32[]{:S(2)}) copy-start(bf16[256,2048]{1,0:T(8,128)(2,1)} %constant.8.clone) | copy-start | bytes 3145732
  4.0 19.6 %copy-start.4 = (f32[2,64]{1,0:T(2,128)S(1)}, f32[2,64]{1,0:T(2,128)}, u32[]{:S(2)}) copy-start(f32[2,64]{1,0:T(2,128)} %param.21) | copy-start | bytes 1540
  23.6 0.7 copy-start.3
  72.1 2.4 %copy-start.2 = (bf16[64,64,128]{2,1,0:T(8,128)(2,1)S(1)}, bf16[64,64,128]{2,1,0:T(8,128)(2,1)}, u32[]{:S(2)}) copy-start(bf16[64,64,128]{2,1,0:T(8,128)(2,1)} %get-tuple-element.97) | copy-start | bytes 3145732

commit v4 on v3

--- a/solution.py
+++ b/solution.py
@@ -11,12 +11,11 @@
 BF = jnp.bfloat16
 F32 = jnp.float32
 MESH = pl.DeviceIdType.MESH
-VMEM_BYTES = 48 << 20
+VMEM_BYTES = 58 << 20
 SIDE = 1024
 ROWS, COLS = 16, 8
 TR, TC = 64, 128
 
-vmem = pl.BlockSpec(memory_space=pltpu.VMEM)
 anywhere = pl.BlockSpec(memory_space=pl.ANY)
 
 
@@ -82,43 +81,96 @@
     return jnp.concatenate([first, c[:, :64]], axis=1)
 
 
-def gather_kernel(coarse_feats, fine_feats, prior, tile, rows, rim_left, rim_right, gathered,
-                  feats, left, right, send, recv, send_a, recv_a, send_b, recv_b, own):
+def chosen_bins(gathered, first, ring):
+    lanes = 256 if ring else 128
+    shape = (SIDE, lanes)
+    wanted = first + (column_offsets(shape) if ring else lanes_of(shape))
+    picked = lax.broadcasted_iota(jnp.int32, shape, 0) == wanted
+    return lax.dot_general(
+        gathered,
+        jnp.where(picked, 1.0, 0.0).astype(BF),
+        (((0,), (0,)), ((), ())),
+        preferred_element_type=F32,
+    )
+
+
+def spread_tables():
+    lane = np.arange(128)
+    source = np.arange(128)[:, None]
+    main = np.stack([source == 64 * k + lane[None] // 2 for k in range(2)])
+    rim = np.zeros((256, 16, 128), bool)
+    for k in range(16):
+        rim[:128, k] = (source == 8 * k + lane[None] // 2) & (lane[None] < 16)
+        rim[128:, k] = (source == 8 * k + (lane[None] - 112) // 2) & (lane[None] >= 112)
+    return main.astype(np.float32), rim.reshape(256, 2048).astype(np.float32)
+
+
+def decoder_kernel(half, coarse_feats, fine_feats, prior, coarse_weights, first_weights,
+                   second_weights, coarse_biases, refine_biases, tables_main, tables_rim,
+                   map_result, refined_result,
+                   whole, weights, first_refine, second_refine, coarse_bias, refine_bias,
+                   main_table, rim_table,
+                   tile, rows, rim_left, rim_right, left, right, feats, gathered, map_out, refined,
+                   x, taps1, hidden, taps2, fields, taps3, w3, bias, fr, fc, fine_r, fine_c, pieces,
+                   got, sides, top, bottom, side_in, wide, fine, taps4, row_terms, row_part,
+                   send, recv, own, send_n, recv_n,
+                   load, send_f, recv_f, send_a, recv_a, send_b, recv_b):
+    loads = [
+        (prior, whole),
+        (coarse_feats, feats.at[0]),
+        (fine_feats, feats.at[1]),
+        (coarse_weights, weights),
+        (first_weights, first_refine),
+        (second_weights, second_refine),
+        (coarse_biases, coarse_bias),
+        (refine_biases, refine_bias),
+        (tables_main, main_table),
+        (tables_rim, rim_table),
+    ]
+    loads = [pltpu.make_async_copy(s, d, load.at[k]) for k, (s, d) in enumerate(loads)]
+    for y in loads:
+        y.start()
     r, c = lax.axis_index("row"), lax.axis_index("col")
+    base_r, base_c = half * (ROWS // 2), half * (COLS // 2)
     up, down = lax.rem(r + ROWS - 1, ROWS), lax.rem(r + 1, ROWS)
     west, east = lax.rem(c + COLS - 1, COLS), lax.rem(c + 1, COLS)
     has_up, has_down, has_west, has_east = r > 0, r < ROWS - 1, c > 0, c < COLS - 1
+    from_r, from_c = base_r + r // 2, base_c + c // 2
+    remote_main = (from_r != r) | (from_c != c)
+    is_source = (r >= base_r) & (r < base_r + ROWS // 2) & (c >= base_c) & (c < base_c + COLS // 2)
+    local_r, local_c = r - base_r, c - base_c
+
+    def main_to(t, h):
+        return 2 * local_r + t, 2 * local_c + h
+
+    def away(to):
+        return (to[0] != r) | (to[1] != c)
+
     barrier = pltpu.get_barrier_semaphore()
 
     def greet(to):
         pl.semaphore_signal(barrier, 1, device_id=to, device_id_type=MESH)
 
+    around = [
+        ((up, c), has_up),
+        ((down, c), has_down),
+        ((r, west), has_west),
+        ((r, east), has_east),
+        ((up, west), has_up & has_west),
+        ((up, east), has_up & has_east),
+        ((down, west), has_down & has_west),
+        ((down, east), has_down & has_east),
+    ]
+    met = around[4:] + [((from_r, from_c), remote_main)]
+    met += [(main_to(t, k), is_source & away(main_to(t, k))) for t in range(2) for k in range(2)]
     for d in range(1, COLS):
         greet((r, lax.rem(c + d, COLS)))
     for d in range(1, ROWS):
         greet((lax.rem(r + d, ROWS), c))
     peers = COLS - 1 + ROWS - 1
-    for a, has_a in ((up, has_up), (down, has_down)):
-        for b, has_b in ((west, has_west), (east, has_east)):
-            pl.when(has_a & has_b)(functools.partial(greet, (a, b)))
-            peers = peers + jnp.where(has_a & has_b, 1, 0)
-
-    both = jnp.concatenate([coarse_feats[...], fine_feats[...]], axis=0).astype(F32)
-    feats[...] = jnp.transpose(both).astype(BF)
-    for q in range(4):
-        tile[16 * q : 16 * q + 16] = jnp.swapaxes(prior[:, 16 * q : 16 * q + 16, :], 0, 1)
-    part = lanes_of((64, 128)) // 16
-
-    def pack(q, carry):
-        low = tile[8 * q]
-        high = pltpu.roll(low, 16, 1)
-        for k in range(1, 8):
-            x = tile[8 * q + k]
-            low = jnp.where(part == k, pltpu.roll(x, 16 * k, 1), low)
-            high = jnp.where(part == k, pltpu.roll(x, (16 * k + 16) % 128, 1), high)
-        left[q] = low
-        right[q] = high
-        return carry
+    for to, there in met:
+        pl.when(there)(functools.partial(greet, to))
+        peers = peers + jnp.where(there, 1, 0)
 
     def copy(source, target, out_sem, in_sem, to):
         return pltpu.make_async_remote_copy(
@@ -130,18 +182,51 @@
             device_id_type=MESH,
         )
 
+    def piece(j, k):
+        t, q = j // 2, lax.rem(j, 2)
+        return copy(pieces.at[k, t, pl.ds(8 * q, 8)], got.at[pl.ds(8 * q, 8)],
+                    send.at[2 * j + k], recv.at[q], main_to(t, k))
+
+    def stay(j, k):
+        t, q = j // 2, lax.rem(j, 2)
+        return pltpu.make_async_copy(
+            pieces.at[k, t, pl.ds(8 * q, 8)], got.at[pl.ds(8 * q, 8)], own.at[q]
+        )
+
+    for y in loads[1:]:
+        y.wait()
+    joined = first_refine[...].reshape(192, 384)
+    w3[...] = halves_joined(joined[:, 0:128], joined[:, 128:256], joined[:, 256:384], False)
+    bias[0] = bias_columns(coarse_bias, 0, 256)
+    bias[1] = bias_columns(coarse_bias, 1, 256)
+    place = r * COLS + c
+    gathered[place] = jnp.concatenate([feats[0], feats[1]], axis=1)
+    loads[0].wait()
+    for q in range(4):
+        tile[16 * q : 16 * q + 16] = jnp.swapaxes(whole[:, 16 * q : 16 * q + 16, :], 0, 1)
     pl.semaphore_wait(barrier, peers)
-    place = r * COLS + c
-    mine = pltpu.make_async_copy(feats, gathered.at[place], own)
-    mine.start()
     first = [
-        copy(feats, gathered.at[place], send_a.at[d], recv_a.at[d], (r, lax.rem(c + d, COLS)))
+        copy(gathered.at[place], gathered.at[place], send_a.at[d], recv_a.at[d],
+             (r, lax.rem(c + d, COLS)))
         for d in range(1, COLS)
     ]
-    for x in first:
-        x.start()
-    lax.fori_loop(0, 8, pack, 0)
-    rims = [
+    for y in first:
+        y.start()
+    sixteenth = lanes_of((64, 128)) // 16
+
+    def pack_edges(q, carry):
+        low = tile[8 * q]
+        high = pltpu.roll(low, 16, 1)
+        for k in range(1, 8):
+            v = tile[8 * q + k]
+            low = jnp.where(sixteenth == k, pltpu.roll(v, 16 * k, 1), low)
+            high = jnp.where(sixteenth == k, pltpu.roll(v, (16 * k + 16) % 128, 1), high)
+        left[q] = low
+        right[q] = high
+        return carry
+
+    lax.fori_loop(0, 8, pack_edges, 0)
+    outlines = [
         (right, rim_left.at[pl.ds(2, 8)], (r, east), has_east, has_west),
         (left, rim_right.at[pl.ds(2, 8)], (r, west), has_west, has_east),
         (tile.at[pl.ds(54, 10)], rows.at[0], (down, c), has_down, has_up),
@@ -155,159 +240,34 @@
         (left.at[pl.ds(0, 2)], rim_right.at[pl.ds(10, 2)], (up, west),
          has_up & has_west, has_down & has_east),
     ]
-    rims = [
-        (copy(s, t, send.at[k], recv.at[k], to), out, into)
-        for k, (s, t, to, out, into) in enumerate(rims)
-    ]
-    for x, out, _ in rims:
-        pl.when(out)(x.start)
-    mine.wait()
-    for x in first:
-        x.wait_recv()
+    outlines = [
+        (copy(s, t, send_f.at[k], recv_f.at[k], to), out, into)
+        for k, (s, t, to, out, into) in enumerate(outlines)
+    ]
+    for y, out, _ in outlines:
+        pl.when(out)(y.start)
+    for y in first:
+        y.wait_recv()
     block = gathered.at[pl.ds(r * COLS, COLS)]
     second = [
         copy(block, block, send_b.at[d], recv_b.at[d], (lax.rem(r + d, ROWS), c))
         for d in range(1, ROWS)
     ]
-    for x in second:
-        x.start()
-    for x in first:
-        x.wait_send()
-    for x, out, into in rims:
-        pl.when(out)(x.wait_send)
-        pl.when(into)(x.wait_recv)
-    for x in second:
-        x.wait()
-
-
-def gather(coarse_feats, fine_feats, prior):
-    return pl.pallas_call(
-        gather_kernel,
-        out_shape=(
-            jax.ShapeDtypeStruct((TR, 64, TC), BF),
-            jax.ShapeDtypeStruct((2, 10, 64, TC), BF),
-            jax.ShapeDtypeStruct((12, 64, TC), BF),
-            jax.ShapeDtypeStruct((12, 64, TC), BF),
-            jax.ShapeDtypeStruct((ROWS * COLS, 8, TC), BF),
-        ),
-        in_specs=[vmem] * 3,
-        out_specs=(vmem,) + (anywhere,) * 4,
-        scratch_shapes=[
-            pltpu.VMEM((8, TC), BF),
-            pltpu.VMEM((8, 64, TC), BF),
-            pltpu.VMEM((8, 64, TC), BF),
-            pltpu.SemaphoreType.DMA((8,)),
-            pltpu.SemaphoreType.DMA((8,)),
-            pltpu.SemaphoreType.DMA((COLS,)),
-            pltpu.SemaphoreType.DMA((COLS,)),
-            pltpu.SemaphoreType.DMA((ROWS,)),
-            pltpu.SemaphoreType.DMA((ROWS,)),
-            pltpu.SemaphoreType.DMA,
-        ],
-        compiler_params=pltpu.CompilerParams(
-            collective_id=1, has_side_effects=True, vmem_limit_bytes=VMEM_BYTES
-        ),
-    )(coarse_feats, fine_feats, prior)
-
-
-def chosen_bins(gathered, first, ring):
-    lanes = 256 if ring else 128
-    shape = (SIDE, lanes)
-    wanted = first + (column_offsets(shape) if ring else lanes_of(shape))
-    picked = lax.broadcasted_iota(jnp.int32, shape, 0) == wanted
-    return lax.dot_general(
-        gathered[...],
-        jnp.where(picked, 1.0, 0.0).astype(BF),
-        (((0,), (0,)), ((), ())),
-        preferred_element_type=F32,
-    )
-
-
-def spread_tables():
-    lane = np.arange(128)
-    source = np.arange(128)[:, None]
-    main = np.stack([source == 64 * k + lane[None] // 2 for k in range(2)])
-    rim = np.zeros((256, 16, 128), bool)
-    for k in range(16):
-        rim[:128, k] = (source == 8 * k + lane[None] // 2) & (lane[None] < 16)
-        rim[128:, k] = (source == 8 * k + (lane[None] - 112) // 2) & (lane[None] >= 112)
-    return main.astype(np.float32), rim.reshape(256, 2048).astype(np.float32)
-
-
-def decoder_kernel(half, tile, rows, rim_left, rim_right, gathered, weights, first_refine,
-                   second_refine, coarse_bias, refine_bias, main_table, rim_table,
-                   map_out, refined,
-                   x, taps1, hidden, taps2, fields, taps3, w3, bias, fr, fc, pieces,
-                   got, sides, top, bottom, side_in, wide, fine, taps4, row_terms, row_part,
-                   send, recv, own, send_n, recv_n):
-    r, c = lax.axis_index("row"), lax.axis_index("col")
-    base_r, base_c = half * (ROWS // 2), half * (COLS // 2)
-    up, down = lax.rem(r + ROWS - 1, ROWS), lax.rem(r + 1, ROWS)
-    west, east = lax.rem(c + COLS - 1, COLS), lax.rem(c + 1, COLS)
-    has_up, has_down, has_west, has_east = r > 0, r < ROWS - 1, c > 0, c < COLS - 1
-    from_r, from_c = base_r + r // 2, base_c + c // 2
-    remote_main = (from_r != r) | (from_c != c)
-    is_source = (r >= base_r) & (r < base_r + ROWS // 2) & (c >= base_c) & (c < base_c + COLS // 2)
-    local_r, local_c = r - base_r, c - base_c
-
-    def main_to(t, h):
-        return 2 * local_r + t, 2 * local_c + h
-
-    def away(to):
-        return (to[0] != r) | (to[1] != c)
-
-    barrier = pltpu.get_barrier_semaphore()
-
-    def greet(to):
-        pl.semaphore_signal(barrier, 1, device_id=to, device_id_type=MESH)
-
-    around = [
-        ((up, c), has_up),
-        ((down, c), has_down),
-        ((r, west), has_west),
-        ((r, east), has_east),
-        ((up, west), has_up & has_west),
-        ((up, east), has_up & has_east),
-        ((down, west), has_down & has_west),
-        ((down, east), has_down & has_east),
-    ]
-    met = around + [((from_r, from_c), remote_main)]
-    met += [(main_to(t, k), is_source & away(main_to(t, k))) for t in range(2) for k in range(2)]
-    peers = 0
-    for to, there in met:
-        pl.when(there)(functools.partial(greet, to))
-        peers = peers + jnp.where(there, 1, 0)
-
-    def copy(source, target, out_sem, in_sem, to):
-        return pltpu.make_async_remote_copy(
-            src_ref=source,
-            dst_ref=target,
-            send_sem=out_sem,
-            recv_sem=in_sem,
-            device_id=to,
-            device_id_type=MESH,
-        )
-
-    def piece(j, k):
-        t, q = j // 2, lax.rem(j, 2)
-        return copy(pieces.at[k, t, pl.ds(8 * q, 8)], got.at[pl.ds(8 * q, 8)],
-                    send.at[2 * j + k], recv.at[q], main_to(t, k))
-
-    def stay(j, k):
-        t, q = j // 2, lax.rem(j, 2)
-        return pltpu.make_async_copy(
-            pieces.at[k, t, pl.ds(8 * q, 8)], got.at[pl.ds(8 * q, 8)], own.at[q]
-        )
-
+    for y in second:
+        y.start()
+    for y in second:
+        y.wait_recv()
+
+    row0, col0 = r * TR, c * TC
+    every_bin = gathered[...].reshape(SIDE, 128)
+    picked = chosen_bins(every_bin, row0 - 24, False)
+    fr[...] = picked[0:64]
+    fine_r[...] = picked[64:128].astype(BF)
+    picked = chosen_bins(every_bin, col0, True)
+    fc[...] = picked[0:64]
+    fine_c[...] = picked[64:128].astype(BF)
     w1 = weights[0].reshape(192, 192)
     w2 = weights[1].reshape(192, 192)
-    joined = first_refine[...].reshape(192, 384)
-    w3[...] = halves_joined(joined[:, 0:128], joined[:, 128:256], joined[:, 256:384], False)
-    bias[0] = bias_columns(coarse_bias, 0, 256)
-    bias[1] = bias_columns(coarse_bias, 1, 256)
-    row0, col0 = r * TR, c * TC
-    fr[...] = chosen_bins(gathered, row0 - 16, False)[0:64]
-    fc[...] = chosen_bins(gathered, col0, True)[0:64]
     cols = col0 + column_offsets((64, 256))
     in_cols = (cols >= 0) & (cols < SIDE)
     half_c, half_r = lax.rem(c, COLS // 2) * TC, lax.rem(r, ROWS // 2) * TR
@@ -328,7 +288,7 @@
         x[at] = jnp.where(inside, value, 0.0).astype(BF)
 
     def features_at(q):
-        return pltpu.roll(fr[...], lax.rem(256 - 8 * q, 128), 1)
+        return pltpu.roll(fr[...], lax.rem(248 - 8 * q, 128), 1)
 
     def rim_rows(side):
         for k in range(10):
@@ -366,6 +326,11 @@
             pieces[0, t, at] = jnp.where(low_half, v, pltpu.roll(u, 64, 1))
             pieces[1, t, at] = jnp.where(low_half, pltpu.roll(v, 64, 1), u)
 
+    for y in first + second:
+        y.wait_send()
+    for y, out, into in outlines:
+        pl.when(out)(y.wait_send)
+        pl.when(into)(y.wait_recv)
     rim_rows(0)
 
     def early_rows(g, carry):
@@ -378,8 +343,6 @@
     tap_products(w2, hidden, 0, taps2, 8, 16, 8, 4, 256)
     field_rows(0, 8, 8)
     tap_products(w3[...], fields, 0, taps3, 16, 8, 8, 4, 128)
-    pl.semaphore_wait(barrier, peers)
-
     def chunk(j, carry):
         @pl.when((j == 1) | (j == 2))
         def _():
@@ -409,6 +372,9 @@
             fields[4 + 16 * q : 20 + 16 * q, :, 0:128], 0, 1
         )
 
+    store_map = pltpu.make_async_copy(map_out, map_result, load.at[0])
+    store_map.start()
+
     wq = halves_joined(joined[:, 0:128], joined[:, 128:256], joined[:, 256:384], True)
     wp = jnp.concatenate(
         [
@@ -418,14 +384,12 @@
         axis=0,
     )
     w4 = second_refine[...].reshape(192, 192)
-    fine_c = chosen_bins(gathered, col0, True)[64:128].astype(BF)
-    terms = jnp.dot(wq, shifted_stack(fine_c, 8, 256), preferred_element_type=F32)
+    terms = jnp.dot(wq, shifted_stack(fine_c[...], 8, 256), preferred_element_type=F32)
     base = terms[64:128] + bias_columns(refine_bias, 0, 256)
     row_terms[0] = base + terms[0:64] + terms[128:192]
     row_terms[1] = base + terms[128:192]
     row_terms[2] = base + terms[0:64]
-    fine_r = chosen_bins(gathered, row0 - 24, False)[64:128].astype(BF)
-    stack = jnp.concatenate([pltpu.roll(fine_r, 8, 1), fine_r, pltpu.roll(fine_r, 120, 1)], axis=0)
+    stack = jnp.concatenate([pltpu.roll(fine_r[...], 8, 1), fine_r[...], pltpu.roll(fine_r[...], 120, 1)], axis=0)
     terms = jnp.dot(wp, stack, preferred_element_type=F32)
     row_part[0] = terms[0:64] + terms[64:128] + terms[128:192]
     row_part[1] = terms[64:128] + jnp.where(c == 0, terms[128:192], terms[0:64])
@@ -547,19 +511,40 @@
             ]
         )
         refined[:, 16 * g : 16 * g + 16, :] = jnp.swapaxes(value, 0, 1)
-
-
-def decoder(half, tile, rows, rim_left, rim_right, gathered, weights, first_refine,
-            second_refine, coarse_bias, refine_bias, main_table, rim_table):
+    store_refined = pltpu.make_async_copy(refined, refined_result, load.at[1])
+    store_refined.start()
+    store_map.wait()
+    store_refined.wait()
+
+
+def decoder(half, *arguments):
     return pl.pallas_call(
         functools.partial(decoder_kernel, half),
         out_shape=(
             jax.ShapeDtypeStruct((64, TR, TC), BF),
             jax.ShapeDtypeStruct((64, TR, TC), BF),
         ),
-        in_specs=[vmem] * 12,
-        out_specs=(vmem, vmem),
+        in_specs=[anywhere] * 10,
+        out_specs=(anywhere, anywhere),
         scratch_shapes=[
+            pltpu.VMEM((64, TR, TC), BF),
+            pltpu.VMEM((2, 3, 64, 192), BF),
+            pltpu.VMEM((3, 64, 384), BF),
+            pltpu.VMEM((3, 64, 192), BF),
+            pltpu.VMEM((2, 64), F32),
+            pltpu.VMEM((2, 64), F32),
+            pltpu.VMEM((2, 128, 128), BF),
+            pltpu.VMEM((256, 2048), BF),
+            pltpu.VMEM((TR, 64, TC), BF),
+            pltpu.VMEM((2, 10, 64, TC), BF),
+            pltpu.VMEM((12, 64, TC), BF),
+            pltpu.VMEM((12, 64, TC), BF),
+            pltpu.VMEM((8, 64, TC), BF),
+            pltpu.VMEM((8, 64, TC), BF),
+            pltpu.VMEM((2, 8, 64), BF),
+            pltpu.VMEM((ROWS * COLS, 8, TC), BF),
+            pltpu.VMEM((64, TR, TC), BF),
+            pltpu.VMEM((64, TR, TC), BF),
             pltpu.VMEM((84, 64, 256), BF),
             pltpu.VMEM((20, 192, 256), F32),
             pltpu.VMEM((80, 64, 256), BF),
@@ -570,6 +555,8 @@
             pltpu.VMEM((2, 64, 256), F32),
             pltpu.VMEM((64, 128), F32),
             pltpu.VMEM((64, 256), F32),
+            pltpu.VMEM((64, 128), BF),
+            pltpu.VMEM((64, 256), BF),
             pltpu.VMEM((2, 2, 16, 64, 128), BF),
             pltpu.VMEM((16, 64, 128), BF),
             pltpu.VMEM((2, 2, 64, 128), BF),
@@ -586,25 +573,29 @@
             pltpu.SemaphoreType.DMA((2,)),
             pltpu.SemaphoreType.DMA((8,)),
             pltpu.SemaphoreType.DMA((8,)),
+            pltpu.SemaphoreType.DMA((10,)),
+            pltpu.SemaphoreType.DMA((8,)),
+            pltpu.SemaphoreType.DMA((8,)),
+            pltpu.SemaphoreType.DMA((COLS,)),
+            pltpu.SemaphoreType.DMA((COLS,)),
+            pltpu.SemaphoreType.DMA((ROWS,)),
+            pltpu.SemaphoreType.DMA((ROWS,)),
         ],
         compiler_params=pltpu.CompilerParams(
             collective_id=2 + half, has_side_effects=True, vmem_limit_bytes=VMEM_BYTES
         ),
-    )(tile, rows, rim_left, rim_right, gathered, weights, first_refine,
-      second_refine, coarse_bias, refine_bias, main_table, rim_table)
+    )(*arguments)
 
 
 def per_device(coarse_feats, fine_feats, pair_prior, zoom_start, coarse_weights, coarse_bias,
                refine_first, refine_second, refine_bias):
-    *held, gathered = gather(coarse_feats, fine_feats, pair_prior)
-    gathered = gathered.reshape(SIDE, 128)
     main_table, rim_table = spread_tables()
     return lax.cond(
         zoom_start[0] == 0,
         functools.partial(decoder, 0),
         functools.partial(decoder, 1),
-        *held, gathered, coarse_weights, refine_first, refine_second, coarse_bias, refine_bias,
-        jnp.asarray(main_table, BF), jnp.asarray(rim_table, BF),
+        coarse_feats.T, fine_feats.T, pair_prior, coarse_weights, refine_first, refine_second,
+        coarse_bias, refine_bias, jnp.asarray(main_table, BF), jnp.asarray(rim_table, BF),
     )
 
 

time: 75.7 us -> 71.3 us (0.942)
  the two profiles are of different devices: /device:TPU:18 before, /device:TPU:1 now
where the time goes in v4:
time: 71.3 us; the launch traced here: 71.1 us
  Pallas kernels  66.9 us (94%)
  local copies, waits for them, and re-layouts  3.28 us (5%)
  between operations  0.72 us (1%)
    pallas_call x1, Pallas kernels, decoder(): pl.pallas_call(functools.partial(decoder_kernel, half), out_shape=(jax.Sh...  66.9 us
    unnamed x12, local copies, waits for them, and re-layouts  3.28 us

profile of v4, /device:TPU:1, one launch (start us, length us, event | category | flops | bytes accessed | tf_op | source)
XLA Modules:
  0.0 71.1 jit_solution(8078276210354600322)
XLA Ops:
  0.6 0.0 copy-start.4
  0.6 0.6 copy-done.4
  1.3 0.0 copy-start.3
  1.3 0.0 copy-start.1
  1.4 0.0 copy-start
  1.4 0.0 copy-start.2
  1.4 0.6 copy-done.3
  2.0 0.0 copy-done.1
  2.0 0.0 copy-done
  2.0 0.0 copy-done.2
  2.1 67.1 %conditional.1 = ((bf16[64,64,128]{2,1,0:T(8,128)(2,1)S(1)}, bf16[64,64,128]{2,1,0:T(8,128)(2,1)S(1)})) conditional(s32[]{:T(128)} %bitcast, (bf16[8,64]{1,0:T(8,128)(2,1)S(1)}, bf16[8,64]{1,0:T(8,128)(2,1)S(1)}, bf16[64,64,128]{2,1,0:T(8,128)(2,1)}, bf16[2,3,64,192]{3,2,1,0:T(8,128)(2,1)}, bf16[3,64,384]{2,1,0:T(8,128)(2,1)}, ...), branch_computations={%region_0.0_spmd.clone, %region_1.0_spmd.clone} | conditional | bytes 8 | solution.py:593
  2.1 66.9 %branch_0_fun.1 = (bf16[64,64,128]{2,1,0:T(8,128)(2,1)S(1)}, bf16[64,64,128]{2,1,0:T(8,128)(2,1)S(1)}) custom-call(bf16[8,64]{1,0:T(8,128)(2,1)S(1)} %get-tuple-element.100.coarse_feats, bf16[8,64]{1,0:T(8,128)(2,1)S(1)} %get-tuple-element.101.fine_feats, bf16[64,64,128]{2,1,0:T(8,128)(2,1)} %get-tuple-element.104.prior, ...), custom_call_target="tpu_custom_call" | custom-call | tf_op jit(solution)/shard_map/cond/branch_0_fun/pallas_call | solution.py:521
  69.2 1.0 %copy.59 = bf16[64,64,128]{2,1,0:T(8,128)(2,1)} copy(bf16[64,64,128]{2,1,0:T(8,128)(2,1)S(1)} %get-tuple-element.142) | data formatting | bytes 2097152
  70.2 1.0 %copy.60 = bf16[64,64,128]{2,1,0:T(8,128)(2,1)} copy(bf16[64,64,128]{2,1,0:T(8,128)(2,1)S(1)} %get-tuple-element.143) | data formatting | bytes 2097152
Async XLA Ops:
  0.6 0.7 copy-start.4
  1.3 0.7 copy-start.3
  1.3 0.7 copy-start.1
  1.4 0.7 copy-start
  1.4 0.7 copy-start.2

commit v5 on v4

--- a/solution.py
+++ b/solution.py
@@ -51,11 +51,11 @@
 
 
 def carry_taps(target, spacing):
-    last = target.shape[0] - 2 * spacing
     for t in range(2 * spacing):
-        target[t, 0:64] = target[last + t, 0:64]
+        last = target.shape[0] - 2 * spacing + t
+        target[last - 8, 0:64] = target[last, 0:64]
         if t >= spacing:
-            target[t, 64:128] = target[last + t, 64:128]
+            target[last - 8, 64:128] = target[last, 64:128]
 
 
 def tap_sum(target, i, spacing, width):
@@ -146,6 +146,7 @@
     def away(to):
         return (to[0] != r) | (to[1] != c)
 
+    gathered[...] = jnp.zeros(gathered.shape, BF)
     barrier = pltpu.get_barrier_semaphore()
 
     def greet(to):
@@ -165,9 +166,16 @@
     met += [(main_to(t, k), is_source & away(main_to(t, k))) for t in range(2) for k in range(2)]
     for d in range(1, COLS):
         greet((r, lax.rem(c + d, COLS)))
+    peers = COLS - 1
+
+    def gives(a, b):
+        return ((a >= 2 * c - 1) & (a <= 2 * c + 2)) | (a == b + 1) | (a == b - 1)
+
     for d in range(1, ROWS):
-        greet((lax.rem(r + d, ROWS), c))
-    peers = COLS - 1 + ROWS - 1
+        other = lax.rem(r + d, ROWS)
+        there = gives(r, other) | gives(other, r)
+        pl.when(there)(functools.partial(greet, (other, c)))
+        peers = peers + jnp.where(there, 1, 0)
     for to, there in met:
         pl.when(there)(functools.partial(greet, to))
         peers = peers + jnp.where(there, 1, 0)
@@ -183,27 +191,20 @@
         )
 
     def piece(j, k):
-        t, q = j // 2, lax.rem(j, 2)
-        return copy(pieces.at[k, t, pl.ds(8 * q, 8)], got.at[pl.ds(8 * q, 8)],
+        t, q = j // 4, lax.rem(j, 4)
+        return copy(pieces.at[k, t, pl.ds(4 * q, 4)], got.at[pl.ds(4 * q, 4)],
                     send.at[2 * j + k], recv.at[q], main_to(t, k))
 
     def stay(j, k):
-        t, q = j // 2, lax.rem(j, 2)
+        t, q = j // 4, lax.rem(j, 4)
         return pltpu.make_async_copy(
-            pieces.at[k, t, pl.ds(8 * q, 8)], got.at[pl.ds(8 * q, 8)], own.at[q]
+            pieces.at[k, t, pl.ds(4 * q, 4)], got.at[pl.ds(4 * q, 4)], own.at[q]
         )
 
-    for y in loads[1:]:
+    for y in loads[1:3]:
         y.wait()
-    joined = first_refine[...].reshape(192, 384)
-    w3[...] = halves_joined(joined[:, 0:128], joined[:, 128:256], joined[:, 256:384], False)
-    bias[0] = bias_columns(coarse_bias, 0, 256)
-    bias[1] = bias_columns(coarse_bias, 1, 256)
     place = r * COLS + c
     gathered[place] = jnp.concatenate([feats[0], feats[1]], axis=1)
-    loads[0].wait()
-    for q in range(4):
-        tile[16 * q : 16 * q + 16] = jnp.swapaxes(whole[:, 16 * q : 16 * q + 16, :], 0, 1)
     pl.semaphore_wait(barrier, peers)
     first = [
         copy(gathered.at[place], gathered.at[place], send_a.at[d], recv_a.at[d],
@@ -212,6 +213,9 @@
     ]
     for y in first:
         y.start()
+    loads[0].wait()
+    for q in range(4):
+        tile[16 * q : 16 * q + 16] = jnp.swapaxes(whole[:, 16 * q : 16 * q + 16, :], 0, 1)
     sixteenth = lanes_of((64, 128)) // 16
 
     def pack_edges(q, carry):
@@ -253,10 +257,16 @@
         copy(block, block, send_b.at[d], recv_b.at[d], (lax.rem(r + d, ROWS), c))
         for d in range(1, ROWS)
     ]
-    for y in second:
-        y.start()
-    for y in second:
-        y.wait_recv()
+    for d, y in enumerate(second, 1):
+        pl.when(gives(r, lax.rem(r + d, ROWS)))(y.start)
+    for y in loads[3:]:
+        y.wait()
+    joined = first_refine[...].reshape(192, 384)
+    w3[...] = halves_joined(joined[:, 0:128], joined[:, 128:256], joined[:, 256:384], False)
+    bias[0] = bias_columns(coarse_bias, 0, 256)
+    bias[1] = bias_columns(coarse_bias, 1, 256)
+    for d, y in enumerate(second, 1):
+        pl.when(gives(lax.rem(r + ROWS - d, ROWS), r))(y.wait_recv)
 
     row0, col0 = r * TR, c * TC
     every_bin = gathered[...].reshape(SIDE, 128)
@@ -318,16 +328,18 @@
             fields[at] = jnp.where(inside, value, 0.0).astype(BF)
 
     def pack(j):
-        t, q = j // 2, lax.rem(j, 2)
-        for k in range(0, 16, 2):
+        t, q = j // 4, lax.rem(j, 4)
+        for k in range(0, 8, 2):
             v = tap_sum(taps3, k, 4, 128).astype(BF)
             u = tap_sum(taps3, k + 1, 4, 128).astype(BF)
-            at = 8 * q + k // 2
+            at = 4 * q + k // 2
             pieces[0, t, at] = jnp.where(low_half, v, pltpu.roll(u, 64, 1))
             pieces[1, t, at] = jnp.where(low_half, pltpu.roll(v, 64, 1), u)
 
-    for y in first + second:
+    for y in first:
         y.wait_send()
+    for d, y in enumerate(second, 1):
+        pl.when(gives(r, lax.rem(r + d, ROWS)))(y.wait_send)
     for y, out, into in outlines:
         pl.when(out)(y.wait_send)
         pl.when(into)(y.wait_recv)
@@ -337,36 +349,32 @@
         own_rows(g)
         return carry
 
-    lax.fori_loop(0, 4, early_rows, 0)
+    lax.fori_loop(0, 2, early_rows, 0)
     tap_products(w1, x, 0, taps1, 0, 20, 10, 2, 256)
     hidden_rows(0, 0, 16)
-    tap_products(w2, hidden, 0, taps2, 8, 16, 8, 4, 256)
-    field_rows(0, 8, 8)
-    tap_products(w3[...], fields, 0, taps3, 16, 8, 8, 4, 128)
+    tap_products(w2, hidden, 0, taps2, 0, 16, 8, 4, 256)
+    field_rows(0, 0, 8)
+    tap_products(w3[...], fields, 0, taps3, 8, 8, 8, 4, 128)
     def chunk(j, carry):
-        @pl.when((j == 1) | (j == 2))
-        def _():
-            own_rows(2 * j + 2)
-            own_rows(2 * j + 3)
-
-        pl.when(j == 3)(lambda: rim_rows(1))
+        pl.when(j < 6)(lambda: own_rows(j + 2))
+        pl.when(j == 6)(lambda: rim_rows(1))
         carry_taps(taps1, 2)
         carry_taps(taps2, 4)
         carry_taps(taps3, 4)
-        tap_products(w1, x, 20 + 16 * j, taps1, 4, 16, 8, 2, 256)
-        hidden_rows(16 + 16 * j, 0, 16)
-        tap_products(w2, hidden, 16 + 16 * j, taps2, 8, 16, 8, 4, 256)
-        field_rows(8 + 16 * j, 0, 16)
-        tap_products(w3[...], fields, 8 + 16 * j, taps3, 8, 16, 8, 4, 128)
+        tap_products(w1, x, 20 + 8 * j, taps1, 12, 8, 8, 2, 256)
+        hidden_rows(16 + 8 * j, 8, 8)
+        tap_products(w2, hidden, 16 + 8 * j, taps2, 8, 8, 8, 4, 256)
+        field_rows(8 + 8 * j, 0, 8)
+        tap_products(w3[...], fields, 8 + 8 * j, taps3, 8, 8, 8, 4, 128)
         pack(j)
         for k in range(2):
-            pl.when(is_source & away(main_to(j // 2, k)))(lambda k=k: piece(j, k).start())
-            pl.when(is_source & jnp.logical_not(away(main_to(j // 2, k))))(
+            pl.when(is_source & away(main_to(j // 4, k)))(lambda k=k: piece(j, k).start())
+            pl.when(is_source & jnp.logical_not(away(main_to(j // 4, k))))(
                 lambda k=k: stay(j, k).start()
             )
         return carry
 
-    lax.fori_loop(0, 4, chunk, 0)
+    lax.fori_loop(0, 8, chunk, 0)
     for q in range(4):
         map_out[:, 16 * q : 16 * q + 16, :] = jnp.swapaxes(
             fields[4 + 16 * q : 20 + 16 * q, :, 0:128], 0, 1
@@ -404,39 +412,38 @@
             )
             wide[at : at + count, k, :, 0:128] = value.reshape(count, 64, 128).astype(BF)
 
+    rims = [
+        (got.at[pl.ds(0, 4)], bottom, (up, c), has_up, has_down, 0),
+        (sides.at[0, 0], side_in.at[1, 1], (r, west), has_west, has_east, 1),
+        (sides.at[1, 0], side_in.at[0, 1], (r, east), has_east, has_west, 1),
+        (sides.at[0, 0], side_in.at[1, 3], (up, west),
+         has_up & has_west, has_down & has_east, 1),
+        (sides.at[1, 0], side_in.at[0, 3], (up, east),
+         has_up & has_east, has_down & has_west, 1),
+        (got.at[pl.ds(12, 4)], top, (down, c), has_down, has_up, 3),
+        (sides.at[0, 1], side_in.at[1, 2], (r, west), has_west, has_east, 3),
+        (sides.at[1, 1], side_in.at[0, 2], (r, east), has_east, has_west, 3),
+        (sides.at[0, 1], side_in.at[1, 0], (down, west),
+         has_down & has_west, has_up & has_east, 3),
+        (sides.at[1, 1], side_in.at[0, 0], (down, east),
+         has_down & has_east, has_up & has_west, 3),
+    ]
+    rims = [
+        (copy(s, t, send_n.at[k], recv_n.at[k], to), out, into, when)
+        for k, (s, t, to, out, into, when) in enumerate(rims)
+    ]
     part = lanes_of((64, 128)) // 8
-    for q in range(2):
-        pl.when(remote_main)(lambda: piece(q, 0).wait_recv())
-        pl.when(jnp.logical_not(remote_main))(lambda: stay(q, 0).wait())
+
+    def pack_sides(half_tile):
         low = high = None
         for k in range(16):
-            v = got[8 * q + k // 2]
-            first = (8 * k - 64 * (k % 2)) % 128
-            moved, other = pltpu.roll(v, first, 1), pltpu.roll(v, (first - 56) % 128, 1)
+            v = got[8 * half_tile + k // 2]
+            start = (8 * k - 64 * (k % 2)) % 128
+            moved, other = pltpu.roll(v, start, 1), pltpu.roll(v, (start - 56) % 128, 1)
             low = moved if k == 0 else jnp.where(part == k, moved, low)
             high = other if k == 0 else jnp.where(part == k, other, high)
-        sides[0, q] = low
-        sides[1, q] = high
-    rims = [
-        (got.at[pl.ds(12, 4)], top, (down, c), has_down, has_up),
-        (got.at[pl.ds(0, 4)], bottom, (up, c), has_up, has_down),
-        (sides.at[0], side_in.at[1, pl.ds(1, 2)], (r, west), has_west, has_east),
-        (sides.at[1], side_in.at[0, pl.ds(1, 2)], (r, east), has_east, has_west),
-        (sides.at[0, 1], side_in.at[1, 0], (down, west),
-         has_down & has_west, has_up & has_east),
-        (sides.at[1, 1], side_in.at[0, 0], (down, east),
-         has_down & has_east, has_up & has_west),
-        (sides.at[0, 0], side_in.at[1, 3], (up, west),
-         has_up & has_west, has_down & has_east),
-        (sides.at[1, 0], side_in.at[0, 3], (up, east),
-         has_up & has_east, has_down & has_west),
-    ]
-    rims = [
-        (copy(s, t, send_n.at[k], recv_n.at[k], to), out, into)
-        for k, (s, t, to, out, into) in enumerate(rims)
-    ]
-    for y, out, _ in rims:
-        pl.when(out)(y.start)
+        sides[0, half_tile] = low
+        sides[1, half_tile] = high
 
     offsets = column_offsets((64, 256)) + col0
     inside_of = [(offsets >= 0) & (offsets < SIDE)]
@@ -464,12 +471,20 @@
         fine_rows(g, 128)
         return carry
 
-    spread_main(got, 0, 16, 4)
-    lax.fori_loop(2, 10, own_fine_rows, 0)
-    for j in range(4):
+    for q in range(4):
+        pl.when(remote_main)(lambda: piece(q, 0).wait_recv())
+        pl.when(jnp.logical_not(remote_main))(lambda: stay(q, 0).wait())
+        if q % 2:
+            pack_sides(q // 2)
+        for y, out, _, when in rims:
+            if when == q:
+                pl.when(out)(y.start)
+        spread_main(got, 4 * q, 4, 4 + 4 * q)
+        lax.fori_loop(2 + 2 * q, 4 + 2 * q, own_fine_rows, 0)
+    for j in range(8):
         for k in range(2):
-            pl.when(is_source & away(main_to(j // 2, k)))(lambda: piece(j, k).wait_send())
-    for y, out, into in rims:
+            pl.when(is_source & away(main_to(j // 4, k)))(lambda: piece(j, k).wait_send())
+    for y, out, into, _ in rims:
         pl.when(out)(y.wait_send)
         pl.when(into)(y.wait_recv)
     spread_main(top, 0, 4, 0)
@@ -548,9 +563,9 @@
             pltpu.VMEM((84, 64, 256), BF),
             pltpu.VMEM((20, 192, 256), F32),
             pltpu.VMEM((80, 64, 256), BF),
-            pltpu.VMEM((24, 192, 256), F32),
+            pltpu.VMEM((16, 192, 256), F32),
             pltpu.VMEM((72, 64, 256), BF),
-            pltpu.VMEM((24, 192, 128), F32),
+            pltpu.VMEM((16, 192, 128), F32),
             pltpu.VMEM((192, 192), BF),
             pltpu.VMEM((2, 64, 256), F32),
             pltpu.VMEM((64, 128), F32),
@@ -568,11 +583,11 @@
             pltpu.VMEM((96, 192, 128), F32),
             pltpu.VMEM((3, 64, 256), F32),
             pltpu.VMEM((2, 64, 128), F32),
-            pltpu.SemaphoreType.DMA((8,)),
-            pltpu.SemaphoreType.DMA((2,)),
-            pltpu.SemaphoreType.DMA((2,)),
-            pltpu.SemaphoreType.DMA((8,)),
-            pltpu.SemaphoreType.DMA((8,)),
+            pltpu.SemaphoreType.DMA((16,)),
+            pltpu.SemaphoreType.DMA((4,)),
+            pltpu.SemaphoreType.DMA((4,)),
+            pltpu.SemaphoreType.DMA((10,)),
+            pltpu.SemaphoreType.DMA((10,)),
             pltpu.SemaphoreType.DMA((10,)),
             pltpu.SemaphoreType.DMA((8,)),
             pltpu.SemaphoreType.DMA((8,)),

time: 71.3 us -> 64.9 us (0.910)
  the two profiles are of different devices: /device:TPU:1 before, /device:TPU:19 now
where the time goes in v5:
time: 64.9 us; the launch traced here: 64.8 us
  Pallas kernels  60.5 us (93%)
  local copies, waits for them, and re-layouts  3.28 us (5%)
  between operations  0.72 us (1%)
    pallas_call x1, Pallas kernels, decoder(): pl.pallas_call(functools.partial(decoder_kernel, half), out_shape=(jax.Sh...  60.5 us
    unnamed x12, local copies, waits for them, and re-layouts  3.28 us

profile of v5, /device:TPU:19, one launch (start us, length us, event | category | flops | bytes accessed | tf_op | source)
XLA Modules:
  0.0 64.8 jit_solution(1980985224306712489)
XLA Ops:
  0.6 0.0 copy-start.4
  0.6 0.6 copy-done.4
  1.3 0.0 copy-start.3
  1.3 0.0 copy-start.1
  1.4 0.0 copy-start
  1.4 0.0 copy-start.2
  1.4 0.6 copy-done.3
  2.0 0.0 copy-done.1
  2.0 0.0 copy-done
  2.0 0.0 copy-done.2
  2.1 60.8 %conditional.1 = ((bf16[64,64,128]{2,1,0:T(8,128)(2,1)S(1)}, bf16[64,64,128]{2,1,0:T(8,128)(2,1)S(1)})) conditional(s32[]{:T(128)} %bitcast, (bf16[8,64]{1,0:T(8,128)(2,1)S(1)}, bf16[8,64]{1,0:T(8,128)(2,1)S(1)}, bf16[64,64,128]{2,1,0:T(8,128)(2,1)}, bf16[2,3,64,192]{3,2,1,0:T(8,128)(2,1)}, bf16[3,64,384]{2,1,0:T(8,128)(2,1)}, ...), branch_computations={%region_0.0_spmd.clone, %region_1.0_spmd.clone} | conditional | bytes 8 | solution.py:608
  2.1 60.5 %branch_1_fun.1 = (bf16[64,64,128]{2,1,0:T(8,128)(2,1)S(1)}, bf16[64,64,128]{2,1,0:T(8,128)(2,1)S(1)}) custom-call(bf16[8,64]{1,0:T(8,128)(2,1)S(1)} %get-tuple-element.118.coarse_feats, bf16[8,64]{1,0:T(8,128)(2,1)S(1)} %get-tuple-element.119.fine_feats, bf16[64,64,128]{2,1,0:T(8,128)(2,1)} %get-tuple-element.122.prior, ...), custom_call_target="tpu_custom_call" | custom-call | tf_op jit(solution)/shard_map/cond/branch_1_fun/pallas_call | solution.py:536
  62.8 1.0 %copy.59 = bf16[64,64,128]{2,1,0:T(8,128)(2,1)} copy(bf16[64,64,128]{2,1,0:T(8,128)(2,1)S(1)} %get-tuple-element.142) | data formatting | bytes 2097152
  63.8 1.0 %copy.60 = bf16[64,64,128]{2,1,0:T(8,128)(2,1)} copy(bf16[64,64,128]{2,1,0:T(8,128)(2,1)S(1)} %get-tuple-element.143) | data formatting | bytes 2097152
Async XLA Ops:
  0.6 0.7 %copy-start.4 = (s32[2]{0:T(128)S(1)}, s32[2]{0:T(128)}, u32[]{:S(2)}) copy-start(s32[2]{0:T(128)} %param.16) | copy-start | bytes 28
  1.3 0.7 %copy-start.3 = (f32[2,64]{1,0:T(2,128)S(1)}, f32[2,64]{1,0:T(2,128)}, u32[]{:S(2)}) copy-start(f32[2,64]{1,0:T(2,128)} %param.21) | copy-start | bytes 1540
  1.3 0.7 %copy-start.1 = (bf16[64,8]{0,1:T(8,128)(2,1)S(1)}, bf16[64,8]{0,1:T(8,128)(2,1)}, u32[]{:S(2)}) copy-start(bf16[64,8]{0,1:T(8,128)(2,1)} %param.14) | copy-start | bytes 3076
  1.4 0.7 %copy-start = (bf16[64,8]{0,1:T(8,128)(2,1)S(1)}, bf16[64,8]{0,1:T(8,128)(2,1)}, u32[]{:S(2)}) copy-start(bf16[64,8]{0,1:T(8,128)(2,1)} %param.13) | copy-start | bytes 3076
  1.4 0.7 %copy-start.2 = (f32[2,64]{1,0:T(2,128)S(1)}, f32[2,64]{1,0:T(2,128)}, u32[]{:S(2)}) copy-start(f32[2,64]{1,0:T(2,128)} %param.18) | copy-start | bytes 1540

commit v6 on v5

--- a/solution.py
+++ b/solution.py
@@ -336,12 +336,7 @@
             pieces[0, t, at] = jnp.where(low_half, v, pltpu.roll(u, 64, 1))
             pieces[1, t, at] = jnp.where(low_half, pltpu.roll(v, 64, 1), u)
 
-    for y in first:
-        y.wait_send()
-    for d, y in enumerate(second, 1):
-        pl.when(gives(r, lax.rem(r + d, ROWS)))(y.wait_send)
-    for y, out, into in outlines:
-        pl.when(out)(y.wait_send)
+    for y, _, into in outlines:
         pl.when(into)(y.wait_recv)
     rim_rows(0)
 
@@ -481,11 +476,7 @@
                 pl.when(out)(y.start)
         spread_main(got, 4 * q, 4, 4 + 4 * q)
         lax.fori_loop(2 + 2 * q, 4 + 2 * q, own_fine_rows, 0)
-    for j in range(8):
-        for k in range(2):
-            pl.when(is_source & away(main_to(j // 4, k)))(lambda: piece(j, k).wait_send())
-    for y, out, into, _ in rims:
-        pl.when(out)(y.wait_send)
+    for y, _, into, _ in rims:
         pl.when(into)(y.wait_recv)
     spread_main(top, 0, 4, 0)
     spread_main(bottom, 0, 4, 20)
@@ -528,6 +519,17 @@
         refined[:, 16 * g : 16 * g + 16, :] = jnp.swapaxes(value, 0, 1)
     store_refined = pltpu.make_async_copy(refined, refined_result, load.at[1])
     store_refined.start()
+    for y in first:
+        y.wait_send()
+    for d, y in enumerate(second, 1):
+        pl.when(gives(r, lax.rem(r + d, ROWS)))(y.wait_send)
+    for y, out, _ in outlines:
+        pl.when(out)(y.wait_send)
+    for j in range(8):
+        for k in range(2):
+            pl.when(is_source & away(main_to(j // 4, k)))(lambda: piece(j, k).wait_send())
+    for y, out, _, _ in rims:
+        pl.when(out)(y.wait_send)
     store_map.wait()
     store_refined.wait()
 

time: 64.9 us -> 69.1 us (1.065)
  the two profiles are of different devices: /device:TPU:19 before, /device:TPU:1 now
where the time goes in v6:
time: 69.1 us; the launch traced here: 69 us
  Pallas kernels  64.8 us (94%)
  local copies, waits for them, and re-layouts  3.28 us (5%)
  between operations  0.72 us (1%)
    pallas_call x1, Pallas kernels, decoder(): pl.pallas_call(functools.partial(decoder_kernel, half), out_shape=(jax.Sh...  64.8 us
    unnamed x12, local copies, waits for them, and re-layouts  3.28 us

profile of v6, /device:TPU:1, one launch (start us, length us, event | category | flops | bytes accessed | tf_op | source)
XLA Modules:
  0.0 69.0 jit_solution(4540674440170231581)
XLA Ops:
  0.6 0.0 copy-start.4
  0.6 0.6 copy-done.4
  1.3 0.0 copy-start.3
  1.3 0.0 copy-start.1
  1.4 0.0 copy-start
  1.4 0.0 copy-start.2
  1.4 0.6 copy-done.3
  2.0 0.0 copy-done.1
  2.0 0.0 copy-done
  2.0 0.0 copy-done.2
  2.1 65.0 %conditional.1 = ((bf16[64,64,128]{2,1,0:T(8,128)(2,1)S(1)}, bf16[64,64,128]{2,1,0:T(8,128)(2,1)S(1)})) conditional(s32[]{:T(128)} %bitcast, (bf16[8,64]{1,0:T(8,128)(2,1)S(1)}, bf16[8,64]{1,0:T(8,128)(2,1)S(1)}, bf16[64,64,128]{2,1,0:T(8,128)(2,1)}, bf16[2,3,64,192]{3,2,1,0:T(8,128)(2,1)}, bf16[3,64,384]{2,1,0:T(8,128)(2,1)}, ...), branch_computations={%region_0.0_spmd.clone, %region_1.0_spmd.clone} | conditional | bytes 8 | solution.py:610
  2.1 64.8 %branch_0_fun.1 = (bf16[64,64,128]{2,1,0:T(8,128)(2,1)S(1)}, bf16[64,64,128]{2,1,0:T(8,128)(2,1)S(1)}) custom-call(bf16[8,64]{1,0:T(8,128)(2,1)S(1)} %get-tuple-element.100.coarse_feats, bf16[8,64]{1,0:T(8,128)(2,1)S(1)} %get-tuple-element.101.fine_feats, bf16[64,64,128]{2,1,0:T(8,128)(2,1)} %get-tuple-element.104.prior, ...), custom_call_target="tpu_custom_call" | custom-call | tf_op jit(solution)/shard_map/cond/branch_0_fun/pallas_call | solution.py:538
  67.1 1.0 %copy.59 = bf16[64,64,128]{2,1,0:T(8,128)(2,1)} copy(bf16[64,64,128]{2,1,0:T(8,128)(2,1)S(1)} %get-tuple-element.142) | data formatting | bytes 2097152
  68.0 1.0 %copy.60 = bf16[64,64,128]{2,1,0:T(8,128)(2,1)} copy(bf16[64,64,128]{2,1,0:T(8,128)(2,1)S(1)} %get-tuple-element.143) | data formatting | bytes 2097152
Async XLA Ops:
  0.6 0.7 copy-start.4
  1.3 0.7 copy-start.3
  1.3 0.7 copy-start.1
  1.4 0.7 %copy-start = (bf16[64,8]{0,1:T(8,128)(2,1)S(1)}, bf16[64,8]{0,1:T(8,128)(2,1)}, u32[]{:S(2)}) copy-start(bf16[64,8]{0,1:T(8,128)(2,1)} %param.13) | copy-start | bytes 3076
  1.4 0.7 %copy-start.2 = (f32[2,64]{1,0:T(2,128)S(1)}, f32[2,64]{1,0:T(2,128)}, u32[]{:S(2)}) copy-start(f32[2,64]{1,0:T(2,128)} %param.18) | copy-start | bytes 1540
